TPU v7x, 32 devices: a whole 2x2x4 slice. The times are simulated.
32 devices in a mesh: seq: 8 (over y, x, core), chan: 4 (over z).
Axes of the slice: x: 2, y: 2, z: 4, core: 2. Of those that a mesh axis runs over, the one named last changes fastest.
Arguments:
- values_in: bfloat16 [4096, 1024], P(('seq', 'chan')), may hold values from -6 to 6
- gate_in: bfloat16 [4096, 1024], P(('seq', 'chan')), may hold values from -6 to 6
- gate_out: bfloat16 [4096, 1024], P(('seq', 'chan')), may hold values from -6 to 6
- cotangent: bfloat16 [4096, 1024], P(('seq', 'chan')), may hold values from -6 to 6
- filter_spectra: float32 [2, 8, 2, 512, 1024], P(None, 'seq', None, None, 'chan'), may hold values from -4 to 4, as said below
Outputs:
- output: bfloat16 [4096, 1024], P(('seq', 'chan'))
- grad_values: bfloat16 [4096, 1024], P(('seq', 'chan'))
- grad_gate_in: bfloat16 [4096, 1024], P(('seq', 'chan'))
- grad_gate_out: bfloat16 [4096, 1024], P(('seq', 'chan'))
- grad_filter: float32 [2, 8, 2, 512, 1024], P(None, 'seq', None, None, 'chan')
Inputs may be any that keep to these rules, and one draw needn't show every extreme that they name: `filter_spectra`: the spectrum is that of a real filter: the value at frequency 8192 - f is the complex conjugate of the value at f, and the values at frequencies 0 and 4096 are real.
All inputs are finite; a program needn't handle non-finite values.
Results may differ from a plain program's by a relative error of at most 0.001.
Values may be sent and summed in bfloat16 or wider, within the bound.
A program may use at most 128 MiB of HBM per device.

v0:
```python
import math

import jax
import jax.numpy as jnp
import numpy as np
from jax import lax
from jax.sharding import PartitionSpec as P

highest = lax.Precision.HIGHEST


def mirror_list(amount):
    bit_count = amount.bit_length() - 1
    mirror_table = np.zeros(amount, np.int64)
    for number in range(amount):
        result = 0
        for bit_place in range(bit_count):
            if number >> bit_place & 1:
                result = result | 1 << bit_count - 1 - bit_place
        mirror_table[number] = result
    return mirror_table


def reversed_index(position, bit_count):
    outcome = jnp.zeros((), jnp.int32)
    for bit_place in range(bit_count):
        outcome = outcome + (position >> bit_place & 1) * (1 << bit_count - 1 - bit_place)
    return outcome


def complex_turn(block, cosine, sine):
    real_part = block[:, 0]
    imag_part = block[:, 1]
    return jnp.stack(
        [real_part * cosine - imag_part * sine, real_part * sine + imag_part * cosine], axis=1
    )


def shard_matrix(amount, inverse):
    mirror_table = mirror_list(amount)
    counter = np.arange(amount)
    if inverse:
        phase = np.outer(counter, mirror_table) % amount
        angle = 2.0 * math.pi * phase / amount
    else:
        phase = np.outer(mirror_table, counter) % amount
        angle = -2.0 * math.pi * phase / amount
    return (jnp.asarray(np.cos(angle), jnp.float32), jnp.asarray(np.sin(angle), jnp.float32))


def mix_shards(pieces, cosine, sine):
    real_part = pieces[:, 0]
    imag_part = pieces[:, 1]

    def apply_matrix(matrix, data):
        return jnp.einsum("ri,seitk->sertk", matrix, data, precision=highest)

    mixed_real = apply_matrix(cosine, real_part) - apply_matrix(sine, imag_part)
    mixed_imag = apply_matrix(cosine, imag_part) + apply_matrix(sine, real_part)
    return jnp.stack([mixed_real, mixed_imag], axis=1)


def forward_rows_spread(block):
    cosine, sine = shard_matrix(lax.axis_size("seq"), False)
    mixed = mix_shards(
        lax.all_to_all(block[:, :, :, None], "seq", split_axis=4, concat_axis=3, tiled=True),
        cosine,
        sine,
    )
    spread = lax.all_to_all(mixed, "seq", split_axis=3, concat_axis=4, tiled=True)
    return spread[:, :, :, 0]


def inverse_rows_spread(block):
    cosine, sine = shard_matrix(lax.axis_size("seq"), True)
    mixed = mix_shards(
        lax.all_to_all(block[:, :, :, None], "seq", split_axis=4, concat_axis=3, tiled=True),
        cosine,
        sine,
    )
    spread = lax.all_to_all(mixed, "seq", split_axis=3, concat_axis=4, tiled=True)
    return spread[:, :, :, 0]


def small_table(amount, sign):
    counter = jnp.arange(amount, dtype=jnp.int32)
    phase = counter[:, None] * counter[None, :] % amount
    angle = sign * 2.0 * math.pi / amount * phase.astype(jnp.float32)
    return (jnp.cos(angle), jnp.sin(angle))


def factored_transform(real_part, imag_part, sign):
    length = real_part.shape[-2]
    inner = 1 << (length.bit_length() - 1) // 2
    outer = length // inner
    leading = real_part.shape[:-2]
    width = real_part.shape[-1]
    real_grid = real_part.reshape(leading + (outer, inner, width))
    imag_grid = imag_part.reshape(leading + (outer, inner, width))
    cos_outer, sin_outer = small_table(outer, sign)

    def first_pass(matrix, data):
        return jnp.einsum("kt,...tad->...kad", matrix, data, precision=highest)

    step_real = first_pass(cos_outer, real_grid) - first_pass(sin_outer, imag_grid)
    step_imag = first_pass(cos_outer, imag_grid) + first_pass(sin_outer, real_grid)
    outer_index = jnp.arange(outer, dtype=jnp.int32)[:, None]
    inner_index = jnp.arange(inner, dtype=jnp.int32)[None, :]
    twist_phase = outer_index * inner_index % length
    twist_angle = sign * 2.0 * math.pi / length * twist_phase.astype(jnp.float32)
    cos_twist = jnp.cos(twist_angle)[:, :, None]
    sin_twist = jnp.sin(twist_angle)[:, :, None]
    turned_real = step_real * cos_twist - step_imag * sin_twist
    turned_imag = step_real * sin_twist + step_imag * cos_twist
    cos_inner, sin_inner = small_table(inner, sign)

    def second_pass(matrix, data):
        return jnp.einsum("ja,...kad->...jkd", matrix, data, precision=highest)

    final_real = second_pass(cos_inner, turned_real) - second_pass(sin_inner, turned_imag)
    final_imag = second_pass(cos_inner, turned_imag) + second_pass(sin_inner, turned_real)
    return (
        final_real.reshape(leading + (length, width)),
        final_imag.reshape(leading + (length, width)),
    )


def on_device(values_in, gate_in, gate_out, cotangent, filter_spectra):
    values, gates_in, gates_out, incoming = (
        lax.all_to_all(values_in, "chan", split_axis=1, concat_axis=0, tiled=True),
        lax.all_to_all(gate_in, "chan", split_axis=1, concat_axis=0, tiled=True),
        lax.all_to_all(gate_out, "chan", split_axis=1, concat_axis=0, tiled=True),
        lax.all_to_all(cotangent, "chan", split_axis=1, concat_axis=0, tiled=True),
    )
    signal = values.astype(jnp.float32) * gates_in.astype(jnp.float32)
    carried = incoming.astype(jnp.float32) * gates_out.astype(jnp.float32)
    shards = lax.axis_size("seq")
    index = lax.axis_index("seq")
    length = signal.shape[0]
    total = 2 * length * shards
    bit_count = shards.bit_length() - 1
    mirror_index = reversed_index(index, bit_count)
    both = jnp.stack([signal, carried])
    half_angle = -math.pi * index.astype(jnp.float32) / shards
    shifted_real = both * jnp.cos(half_angle)
    shifted_imag = both * jnp.sin(half_angle)
    block = jnp.stack(
        [
            jnp.stack([both, shifted_real], axis=1),
            jnp.stack([jnp.zeros_like(both), shifted_imag], axis=1),
        ],
        axis=1,
    )
    block = forward_rows_spread(block)
    freq_low = 2 * mirror_index + jnp.arange(2, dtype=jnp.int32)
    positions = jnp.arange(length, dtype=jnp.int32)
    twist_phase = freq_low[:, None] * positions[None, :] % total
    twist = 2.0 * math.pi / total * twist_phase.astype(jnp.float32)
    cos_twist = jnp.cos(twist)[:, :, None]
    sin_twist = jnp.sin(twist)[:, :, None]
    block = complex_turn(block, cos_twist, -sin_twist)
    spec_real, spec_imag = factored_transform(block[:, 0], block[:, 1], -1.0)
    sig_real = spec_real[0]
    sig_imag = spec_imag[0]
    car_real = spec_real[1]
    car_imag = spec_imag[1]
    filt_real = filter_spectra[0, 0]
    filt_imag = filter_spectra[1, 0]
    grad_real = (sig_real * car_real + sig_imag * car_imag) / total
    grad_imag = (sig_real * car_imag - sig_imag * car_real) / total
    grad_filter = jnp.stack([grad_real, grad_imag])[:, None]
    prod_real = sig_real * filt_real - sig_imag * filt_imag
    prod_imag = sig_real * filt_imag + sig_imag * filt_real
    back_real = filt_real * car_real + filt_imag * car_imag
    back_imag = filt_real * car_imag - filt_imag * car_real
    packed_real = prod_real - back_imag
    packed_imag = prod_imag + back_real
    inv_real, inv_imag = factored_transform(packed_real, packed_imag, 1.0)
    block = jnp.stack([inv_real, inv_imag])[None]
    block = complex_turn(block, cos_twist, sin_twist)
    block = inverse_rows_spread(block)
    lift = math.pi * index.astype(jnp.float32) / shards
    first_real = block[0, 0, 0]
    first_imag = block[0, 1, 0]
    second_real = block[0, 0, 1]
    second_imag = block[0, 1, 1]
    conv = (first_real + second_real * jnp.cos(lift) - second_imag * jnp.sin(lift)) / total
    back = (first_imag + second_real * jnp.sin(lift) + second_imag * jnp.cos(lift)) / total
    output = (gates_out.astype(jnp.float32) * conv).astype(jnp.bfloat16)
    grad_gate_out = (incoming.astype(jnp.float32) * conv).astype(jnp.bfloat16)
    grad_values = (back * gates_in.astype(jnp.float32)).astype(jnp.bfloat16)
    grad_gate_in = (back * values.astype(jnp.float32)).astype(jnp.bfloat16)
    results = (
        lax.all_to_all(output, "chan", split_axis=0, concat_axis=1, tiled=True),
        lax.all_to_all(grad_values, "chan", split_axis=0, concat_axis=1, tiled=True),
        lax.all_to_all(grad_gate_in, "chan", split_axis=0, concat_axis=1, tiled=True),
        lax.all_to_all(grad_gate_out, "chan", split_axis=0, concat_axis=1, tiled=True),
    )
    return (results[0], results[1], results[2], results[3], grad_filter)


def solution(mesh):
    placed = (
        P(("seq", "chan"), None),
        P(("seq", "chan"), None),
        P(("seq", "chan"), None),
        P(("seq", "chan"), None),
        P(None, "seq", None, None, "chan"),
    )
    return jax.shard_map(
        on_device,
        mesh=mesh,
        in_specs=placed,
        out_specs=(
            P(("seq", "chan"), None),
            P(("seq", "chan"), None),
            P(("seq", "chan"), None),
            P(("seq", "chan"), None),
            P(None, "seq", None, None, "chan"),
        ),
        check_vma=False,
    )
```

profile of v0, /device:TPU:0, one launch (start us, length us, event | category | flops | bytes accessed | tf_op | source)
XLA Modules:
  0.0 345.9 jit_solution(17266646379247616356)
XLA Ops:
  2.5 6.3 %all-to-all-start.1 = ((bf16[128,4,256]{0,2,1:T(8,128)(2,1)}), bf16[128,4,256]{0,2,1:T(8,128)(2,1)S(1)}, u32[]{:S(2)}, u32[]{:S(2)}) async-start(bf16[128,4,256]{0,2,1:T(8,128)(2,1)} %bitcast.2), calls=%async_computation.1 | async-start | bytes 524288 | tf_op jit(solution)/shard_map/all_to_all | solution.py:130
  10.6 7.1 %all-to-all-done.1 = bf16[128,4,256]{0,2,1:T(8,128)(2,1)S(1)} async-done(((bf16[128,4,256]{0,2,1:T(8,128)(2,1)}), bf16[128,4,256]{0,2,1:T(8,128)(2,1)S(1)}, u32[]{:S(2)}, u32[]{:S(2)}) %all-to-all-start.1) | async-done | bytes 262176 | tf_op jit(solution)/shard_map/all_to_all | solution.py:130
  17.8 3.4 all-to-all-start.2
  22.0 6.1 %all-to-all-done.2 = bf16[128,4,256]{0,2,1:T(8,128)(2,1)S(1)} async-done(((bf16[128,4,256]{0,2,1:T(8,128)(2,1)}), bf16[128,4,256]{0,2,1:T(8,128)(2,1)S(1)}, u32[]{:S(2)}, u32[]{:S(2)}) %all-to-all-start.2) | async-done | bytes 262176 | tf_op jit(solution)/shard_map/all_to_all | solution.py:131
  28.2 3.4 all-to-all-start
  32.4 5.9 %all-to-all-done = bf16[128,4,256]{0,2,1:T(8,128)(2,1)S(1)} async-done(((bf16[128,4,256]{0,2,1:T(8,128)(2,1)}), bf16[128,4,256]{0,2,1:T(8,128)(2,1)S(1)}, u32[]{:S(2)}, u32[]{:S(2)}) %all-to-all-start) | async-done | bytes 262176 | tf_op jit(solution)/shard_map/all_to_all | solution.py:132
  38.3 3.4 all-to-all-start.3
  42.2 6.3 %all-to-all-done.3 = bf16[128,4,256]{0,2,1:T(8,128)(2,1)S(1)} async-done(((bf16[128,4,256]{0,2,1:T(8,128)(2,1)}), bf16[128,4,256]{0,2,1:T(8,128)(2,1)S(1)}, u32[]{:S(2)}, u32[]{:S(2)}) %all-to-all-start.3) | async-done | bytes 262176 | tf_op jit(solution)/shard_map/all_to_all | solution.py:133
  50.5 3.2 copy.124
  53.7 52.6 %all_to_all.158 = f32[2,2,2,1,512,256]{5,0,2,1,3,4:T(2,128)S(1)} all-to-all(f32[2,2,2,1,512,256]{5,0,2,1,3,4:T(2,128)S(1)} %copy.124), channel_id=1, replica_groups=mesh['seq'=8,'chan'=4] {'seq'}, dimensions={4} | all-to-all | bytes 8388608 | tf_op jit(solution)/shard_map/all_to_all | solution.py:66
  108.3 3.1 fusion.3
  111.5 3.1 fusion.2
  114.6 3.2 subtract_bitcast_fusion.1
  117.8 3.4 add_bitcast_fusion.1
  121.4 3.3 copy.128
  124.7 4.6 %all-to-all-start.5 = ((f32[2,2,2,8,64,256]{5,4,2,0,1,3:T(8,128)}), f32[2,2,2,8,64,256]{5,4,2,0,1,3:T(8,128)}, u32[]{:S(2)}, u32[]{:S(2)}) async-start(f32[2,2,2,8,64,256]{5,4,2,0,1,3:T(8,128)} %copy.128), calls=%async_computation.5 | async-start | bytes 8388608 | tf_op jit(solution)/shard_map/all_to_all | solution.py:70
  131.5 46.9 %all-to-all-done.5 = f32[2,2,2,8,64,256]{5,4,2,0,1,3:T(8,128)} async-done(((f32[2,2,2,8,64,256]{5,4,2,0,1,3:T(8,128)}), f32[2,2,2,8,64,256]{5,4,2,0,1,3:T(8,128)}, u32[]{:S(2)}, u32[]{:S(2)}) %all-to-all-start.5) | async-done | bytes 4194336 | tf_op jit(solution)/shard_map/all_to_all | solution.py:70
  181.9 3.2 fusion.16
  185.2 3.2 fusion.14
  188.4 3.3 fusion.22
  191.7 4.3 %fusion = (f32[2,2,32,16,256]{4,2,3,1,0:T(8,128)S(1)}, f32[2,2,32,16,256]{4,2,3,1,0:T(8,128)S(1)}) fusion(f32[2,2,16,256,32]{3,4,2,1,0:T(8,128)S(1)} %fusion.22, f32[32,16]{0,1:T(8,128)S(1)} %get-tuple-element.58, f32[32,16]{0,1:T(8,128)S(1)} %get-tuple-element.59, f32[2,2,16,256,32]{3,4,2,1,0:T(8,128)S(1)} %fusion.14, ...), kind=kOutput, calls=%fused_computation.11 | convolution fusion | flops 205010944 | bytes 10489856 | tf_op jit(solution)/shard_map/kt,...tad->...kad/dot_general | solution.py:103
  196.0 3.1 fusion.6
  202.3 3.3 add_bitcast_fusion
  205.6 3.2 subtract_bitcast_fusion
  231.6 29.0 %all_to_all.159 = f32[1,2,2,1,512,256]{5,2,1,3,0,4:T(2,128)S(1)} all-to-all(f32[1,2,2,1,512,256]{5,2,1,3,0,4:T(2,128)S(1)} %copy.152), channel_id=1, replica_groups=mesh['seq'=8,'chan'=4] {'seq'}, dimensions={4} | all-to-all | bytes 4194304 | tf_op jit(solution)/shard_map/all_to_all | solution.py:77
  270.4 3.6 %all-to-all-start.7 = ((f32[1,2,2,8,64,256]{5,4,2,1,0,3:T(8,128)}), f32[1,2,2,8,64,256]{5,4,2,1,0,3:T(8,128)S(1)}, u32[]{:S(2)}, u32[]{:S(2)}) async-start(f32[1,2,2,8,64,256]{5,4,2,1,0,3:T(8,128)} %copy.156), calls=%async_computation.7 | async-start | bytes 4194304 | tf_op jit(solution)/shard_map/all_to_all | solution.py:81
  274.2 26.4 %all-to-all-done.7 = f32[1,2,2,8,64,256]{5,4,2,1,0,3:T(8,128)S(1)} async-done(((f32[1,2,2,8,64,256]{5,4,2,1,0,3:T(8,128)}), f32[1,2,2,8,64,256]{5,4,2,1,0,3:T(8,128)S(1)}, u32[]{:S(2)}, u32[]{:S(2)}) %all-to-all-start.7) | async-done | bytes 2097184 | tf_op jit(solution)/shard_map/all_to_all | solution.py:81
  302.7 10.3 %all_to_all.160 = bf16[4,128,256]{1,2,0:T(8,128)(2,1)S(1)} all-to-all(bf16[4,128,256]{1,2,0:T(8,128)(2,1)S(1)} %get-tuple-element.51), channel_id=1, replica_groups=mesh['seq'=8,'chan'=4] {'chan'}, dimensions={0} | all-to-all | bytes 524288 | tf_op jit(solution)/shard_map/all_to_all | solution.py:195
  313.1 4.2 %all-to-all-start.10 = ((bf16[4,128,256]{1,2,0:T(8,128)(2,1)}), bf16[4,128,256]{1,2,0:T(8,128)(2,1)}, u32[]{:S(2)}, u32[]{:S(2)}) async-start(bf16[4,128,256]{1,2,0:T(8,128)(2,1)} %get-tuple-element.50), calls=%async_computation.10 | async-start | bytes 524288 | tf_op jit(solution)/shard_map/all_to_all | solution.py:196
  319.4 4.7 %all-to-all-done.10 = bf16[4,128,256]{1,2,0:T(8,128)(2,1)} async-done(((bf16[4,128,256]{1,2,0:T(8,128)(2,1)}), bf16[4,128,256]{1,2,0:T(8,128)(2,1)}, u32[]{:S(2)}, u32[]{:S(2)}) %all-to-all-start.10) | async-done | bytes 262176 | tf_op jit(solution)/shard_map/all_to_all | solution.py:196
  324.1 10.7 %all_to_all.161 = bf16[4,128,256]{1,2,0:T(8,128)(2,1)S(1)} all-to-all(bf16[4,128,256]{1,2,0:T(8,128)(2,1)} %get-tuple-element.49), channel_id=1, replica_groups=mesh['seq'=8,'chan'=4] {'chan'}, dimensions={0} | all-to-all | bytes 524288 | tf_op jit(solution)/shard_map/all_to_all | solution.py:194
  334.7 3.4 all-to-all-start.11
  (94 shorter events, 62.9 us)
Async XLA Ops:
  0.6 20.5 %copy-start.7 = (bf16[128,1024]{1,0:T(8,128)(2,1)S(1)}, bf16[128,1024]{1,0:T(8,128)(2,1)}, u32[]{:S(2)}) copy-start(bf16[128,1024]{1,0:T(8,128)(2,1)} %param.11) | copy-start | bytes 786436
  0.6 30.9 %copy-start.8 = (bf16[128,1024]{1,0:T(8,128)(2,1)S(1)}, bf16[128,1024]{1,0:T(8,128)(2,1)}, u32[]{:S(2)}) copy-start(bf16[128,1024]{1,0:T(8,128)(2,1)} %param.12) | copy-start | bytes 786436
  2.5 15.3 %all-to-all-start.1 = ((bf16[128,4,256]{0,2,1:T(8,128)(2,1)}), bf16[128,4,256]{0,2,1:T(8,128)(2,1)S(1)}, u32[]{:S(2)}, u32[]{:S(2)}) async-start(bf16[128,4,256]{0,2,1:T(8,128)(2,1)} %bitcast.2), calls=%async_computation.1 | async-start | bytes 524288 | tf_op jit(solution)/shard_map/all_to_all | solution.py:130
  17.8 10.4 %all-to-all-start.2 = ((bf16[128,4,256]{0,2,1:T(8,128)(2,1)}), bf16[128,4,256]{0,2,1:T(8,128)(2,1)S(1)}, u32[]{:S(2)}, u32[]{:S(2)}) async-start(bf16[128,4,256]{0,2,1:T(8,128)(2,1)} %bitcast.3), calls=%async_computation.2 | async-start | bytes 524288 | tf_op jit(solution)/shard_map/all_to_all | solution.py:131
  28.2 13.8 %copy-start.3 = (bf16[128,4,256]{0,2,1:T(8,128)(2,1)}, bf16[128,4,256]{0,2,1:T(8,128)(2,1)S(1)}, u32[]{:S(2)}) copy-start(bf16[128,4,256]{0,2,1:T(8,128)(2,1)S(1)} %all-to-all-done.2) | copy-start | bytes 786436
  28.2 10.2 %all-to-all-start = ((bf16[128,4,256]{0,2,1:T(8,128)(2,1)}), bf16[128,4,256]{0,2,1:T(8,128)(2,1)S(1)}, u32[]{:S(2)}, u32[]{:S(2)}) async-start(bf16[128,4,256]{0,2,1:T(8,128)(2,1)} %bitcast), calls=%async_computation | async-start | bytes 524288 | tf_op jit(solution)/shard_map/all_to_all | solution.py:132
  38.3 10.2 %copy-start.1 = (bf16[128,4,256]{0,2,1:T(8,128)(2,1)}, bf16[128,4,256]{0,2,1:T(8,128)(2,1)S(1)}, u32[]{:S(2)}) copy-start(bf16[128,4,256]{0,2,1:T(8,128)(2,1)S(1)} %all-to-all-done) | copy-start | bytes 786436
  38.3 10.2 %all-to-all-start.3 = ((bf16[128,4,256]{0,2,1:T(8,128)(2,1)}), bf16[128,4,256]{0,2,1:T(8,128)(2,1)S(1)}, u32[]{:S(2)}, u32[]{:S(2)}) async-start(bf16[128,4,256]{0,2,1:T(8,128)(2,1)} %bitcast.6), calls=%async_computation.3 | async-start | bytes 524288 | tf_op jit(solution)/shard_map/all_to_all | solution.py:133
  48.5 0.7 copy-start.5
  107.6 0.7 copy-start.11
  108.3 3.1 copy-start.12
  124.7 53.7 %all-to-all-start.5 = ((f32[2,2,2,8,64,256]{5,4,2,0,1,3:T(8,128)}), f32[2,2,2,8,64,256]{5,4,2,0,1,3:T(8,128)}, u32[]{:S(2)}, u32[]{:S(2)}) async-start(f32[2,2,2,8,64,256]{5,4,2,0,1,3:T(8,128)} %copy.128), calls=%async_computation.5 | async-start | bytes 8388608 | tf_op jit(solution)/shard_map/all_to_all | solution.py:70
  261.1 0.7 copy-start.10
  261.8 3.3 copy-start.9
  270.4 30.2 %all-to-all-start.7 = ((f32[1,2,2,8,64,256]{5,4,2,1,0,3:T(8,128)}), f32[1,2,2,8,64,256]{5,4,2,1,0,3:T(8,128)S(1)}, u32[]{:S(2)}, u32[]{:S(2)}) async-start(f32[1,2,2,8,64,256]{5,4,2,1,0,3:T(8,128)} %copy.156), calls=%async_computation.7 | async-start | bytes 4194304 | tf_op jit(solution)/shard_map/all_to_all | solution.py:81
  300.7 1.2 copy-start.4
  301.9 16.6 %copy-start.2 = (bf16[128,4,256]{0,2,1:T(8,128)(2,1)S(1)}, bf16[128,4,256]{0,2,1:T(8,128)(2,1)}, u32[]{:S(2)}) copy-start(bf16[128,4,256]{0,2,1:T(8,128)(2,1)} %copy-done.1) | copy-start | bytes 786436
  301.9 16.6 %copy-start.6 = (bf16[128,4,256]{0,2,1:T(8,128)(2,1)S(1)}, bf16[128,4,256]{0,2,1:T(8,128)(2,1)}, u32[]{:S(2)}) copy-start(bf16[128,4,256]{0,2,1:T(8,128)(2,1)} %copy-done.5) | copy-start | bytes 786436
  313.1 25.1 %copy-start = (f32[1,2,16,32,256]{4,2,3,1,0:T(8,128)S(1)}, f32[1,2,16,32,256]{4,2,3,1,0:T(8,128)}, u32[]{:S(2)}) copy-start(f32[1,2,16,32,256]{4,2,3,1,0:T(8,128)} %get-tuple-element.26) | copy-start | bytes 3145732
  313.1 11.0 %all-to-all-start.10 = ((bf16[4,128,256]{1,2,0:T(8,128)(2,1)}), bf16[4,128,256]{1,2,0:T(8,128)(2,1)}, u32[]{:S(2)}, u32[]{:S(2)}) async-start(bf16[4,128,256]{1,2,0:T(8,128)(2,1)} %get-tuple-element.50), calls=%async_computation.10 | async-start | bytes 524288 | tf_op jit(solution)/shard_map/all_to_all | solution.py:196
  334.7 10.2 %all-to-all-start.11 = ((bf16[4,128,256]{1,2,0:T(8,128)(2,1)}), bf16[4,128,256]{1,2,0:T(8,128)(2,1)S(1)}, u32[]{:S(2)}, u32[]{:S(2)}) async-start(bf16[4,128,256]{1,2,0:T(8,128)(2,1)} %get-tuple-element.48), calls=%async_computation.11 | async-start | bytes 524288 | tf_op jit(solution)/shard_map/all_to_all | solution.py:197
where the time goes:
time: 352 us; the launch traced here: 346 us
  waiting for transfers between devices  104 us (30%)
  blocking collectives  103 us (29%)
  matrix products  60.1 us (17%)
  local copies, waits for them, and re-layouts  35.3 us (10%)
  starting transfers between devices  32.3 us (9%)
  other arithmetic  9.93 us (3%)
    all_to_all x1, blocking collectives, forward_rows_spread(): lax.all_to_all(block[:, :, :, None], 'seq', split_axis=4, concat_axis=3,...  52.6 us
    all_to_all x1, waiting for transfers between devices, forward_rows_spread(): lax.all_to_all(mixed, 'seq', split_axis=3, concat_axis=4, tiled=True)  46.9 us
    all_to_all x1, blocking collectives, inverse_rows_spread(): lax.all_to_all(block[:, :, :, None], 'seq', split_axis=4, concat_axis=3,...  29 us
    all_to_all x1, waiting for transfers between devices, inverse_rows_spread(): lax.all_to_all(mixed, 'seq', split_axis=3, concat_axis=4, tiled=True)  26.4 us
    dot_general x8, matrix products, first_pass(): return jnp.einsum('kt,...tad->...kad', matrix, data, precision=highest)  21.7 us
    dot_general x8, matrix products, apply_matrix(): return jnp.einsum('ri,seitk->sertk', matrix, data, precision=highest)  19.3 us
    dot_general x8, matrix products, second_pass(): return jnp.einsum('ja,...kad->...jkd', matrix, data, precision=highest)  19.2 us
    unnamed x34, local copies, waits for them, and re-layouts  11.1 us
  transfers between devices with their start and end apart: 8, of which 8 were waited for; matrix products, arithmetic and copies ran while one was open for 4% of the time, Pallas kernels for 0%

commit v1 on v0

v1 whole, which is shorter than its diff:
```python
import functools
import math

import jax
import jax.numpy as jnp
import numpy as np
from jax import lax
from jax.experimental import pallas as pl
from jax.experimental.pallas import tpu as pltpu
from jax.sharding import PartitionSpec as P

MESH = pl.DeviceIdType.MESH
ANY = pl.BlockSpec(memory_space=pl.ANY)
WHOLE = pl.BlockSpec(memory_space=pltpu.VMEM)


def mirrored(number, bits):
    out = 0
    for place in range(bits):
        out = out + ((number >> place) & 1) * (1 << (bits - 1 - place))
    return out


def meet(peers):
    barrier = pltpu.get_barrier_semaphore()
    for peer in peers:
        pl.semaphore_signal(barrier, inc=1, device_id=peer, device_id_type=MESH)
    pl.semaphore_wait(barrier, len(peers))


def gather_kernel(shards, groups, *refs):
    inputs, held = refs[:4], refs[4]
    own_sem, z_send, z_recv, s_send, s_recv = refs[5:]
    s, c = lax.axis_index("seq"), lax.axis_index("chan")
    width = inputs[0].shape[1] // groups
    bits = shards.bit_length() - 1
    meet([(s, c ^ d) for d in range(1, groups)] + [(s ^ (1 << b), c) for b in range(bits)])

    def columns(group):
        return pl.ds(pl.multiple_of(group * width, width), width)

    crossing = {}
    for d in range(1, groups):
        for a in range(4):
            crossing[d, a] = pltpu.make_async_remote_copy(
                src_ref=inputs[a].at[:, columns(c ^ d)],
                dst_ref=held.at[s, c, a],
                send_sem=z_send.at[d * 4 + a],
                recv_sem=z_recv.at[d * 4 + a],
                device_id=(s, c ^ d),
                device_id_type=MESH,
            )
            crossing[d, a].start()
    own = [
        pltpu.make_async_copy(inputs[a].at[:, columns(c)], held.at[s, c, a], own_sem.at[a])
        for a in range(4)
    ]
    for copy in own:
        copy.start()

    def arrived(d, a):
        return pltpu.make_async_remote_copy(
            src_ref=held.at[s, c ^ d, a],
            dst_ref=held.at[s, c ^ d, a],
            send_sem=z_send.at[d * 4 + a],
            recv_sem=z_recv.at[d * 4 + a],
            device_id=(s, c ^ d),
            device_id_type=MESH,
        )

    def piece(d, owner, slot, partner):
        return pltpu.make_async_remote_copy(
            src_ref=held.at[owner, c ^ d],
            dst_ref=held.at[owner, c ^ d],
            send_sem=s_send.at[d * shards + slot],
            recv_sem=s_recv.at[d * shards + slot],
            device_id=(partner, c),
            device_id_type=MESH,
        )

    far = list(range(1, bits))
    orders = [(far if d % 2 == 0 else far[::-1]) + [0] for d in range(groups)]
    reached = []
    for d in range(groups):
        masks, levels = [0], []
        for b in orders[d]:
            levels.append([(m, m ^ (1 << b), 1 << b) for m in masks])
            masks = masks + [m ^ (1 << b) for m in masks]
        reached.append(levels)
    sent = []
    for tick in range(groups + bits):
        for d in range(groups):
            level = tick - d
            if level < 0 or level > bits:
                continue
            if level == 0:
                if d == 0:
                    for copy in own:
                        copy.wait()
                else:
                    for a in range(4):
                        arrived(d, a).wait_recv()
            else:
                for m, slot, step in reached[d][level - 1]:
                    piece(d, s ^ slot, slot, s ^ step).wait_recv()
            if level < bits:
                for m, slot, step in reached[d][level]:
                    copy = piece(d, s ^ m, slot, s ^ step)
                    copy.start()
                    sent.append(copy)
    for copy in crossing.values():
        copy.wait_send()
    for copy in sent:
        copy.wait_send()


def gather(inputs, shards, groups):
    rows, channels = inputs[0].shape
    return pl.pallas_call(
        functools.partial(gather_kernel, shards, groups),
        out_shape=jax.ShapeDtypeStruct((shards, groups, 4, rows, channels // groups), inputs[0].dtype),
        in_specs=[WHOLE] * 4,
        out_specs=ANY,
        scratch_shapes=[
            pltpu.SemaphoreType.DMA((4,)),
            pltpu.SemaphoreType.DMA((groups * 4,)),
            pltpu.SemaphoreType.DMA((groups * 4,)),
            pltpu.SemaphoreType.DMA((groups * shards,)),
            pltpu.SemaphoreType.DMA((groups * shards,)),
        ],
        compiler_params=pltpu.CompilerParams(collective_id=0, has_side_effects=True),
        name="gather",
    )(*inputs)


def trade_kernel(shards, source, target, own_sem, send_sem, recv_sem):
    s, c = lax.axis_index("seq"), lax.axis_index("chan")
    meet([(s ^ j, c) for j in range(1, shards)])

    def transfer(j):
        return pltpu.make_async_remote_copy(
            src_ref=source.at[s ^ j],
            dst_ref=target.at[s],
            send_sem=send_sem.at[j],
            recv_sem=recv_sem.at[j],
            device_id=(s ^ j, c),
            device_id_type=MESH,
        )

    def landing(j):
        return pltpu.make_async_remote_copy(
            src_ref=source.at[s ^ j],
            dst_ref=target.at[s ^ j],
            send_sem=send_sem.at[j],
            recv_sem=recv_sem.at[j],
            device_id=(s ^ j, c),
            device_id_type=MESH,
        )

    for j in range(shards - 1, 0, -1):
        transfer(j).start()
    own = pltpu.make_async_copy(source.at[s], target.at[s], own_sem)
    own.start()
    own.wait()
    for j in range(1, shards):
        landing(j).wait_recv()
    for j in range(1, shards):
        transfer(j).wait_send()


def trade(block):
    shards = block.shape[0]
    return pl.pallas_call(
        functools.partial(trade_kernel, shards),
        out_shape=jax.ShapeDtypeStruct(block.shape, block.dtype),
        in_specs=[WHOLE],
        out_specs=ANY,
        scratch_shapes=[
            pltpu.SemaphoreType.DMA,
            pltpu.SemaphoreType.DMA((shards,)),
            pltpu.SemaphoreType.DMA((shards,)),
        ],
        compiler_params=pltpu.CompilerParams(collective_id=1, has_side_effects=True),
        name="trade",
    )(block)


def deliver_kernel(shards, groups, source, target, own_sem, send_sem, recv_sem):
    s, c = lax.axis_index("seq"), lax.axis_index("chan")
    peers = [(j, d) for d in range(groups - 1, -1, -1) for j in range(shards) if j or d]
    meet([(s ^ j, c ^ d) for j, d in peers])

    def transfer(j, d, landing):
        to_s, to_c = (s ^ j, c ^ d) if landing else (s, c)
        return pltpu.make_async_remote_copy(
            src_ref=source.at[s ^ j, c ^ d],
            dst_ref=target.at[to_s, to_c],
            send_sem=send_sem.at[d * shards + j],
            recv_sem=recv_sem.at[d * shards + j],
            device_id=(s ^ j, c ^ d),
            device_id_type=MESH,
        )

    for j, d in peers:
        transfer(j, d, False).start()
    own = pltpu.make_async_copy(source.at[s, c], target.at[s, c], own_sem)
    own.start()
    own.wait()
    for j, d in peers:
        transfer(j, d, True).wait_recv()
    for j, d in peers:
        transfer(j, d, False).wait_send()


def deliver(block):
    shards, groups = block.shape[:2]
    return pl.pallas_call(
        functools.partial(deliver_kernel, shards, groups),
        out_shape=jax.ShapeDtypeStruct(block.shape, block.dtype),
        in_specs=[WHOLE],
        out_specs=ANY,
        scratch_shapes=[
            pltpu.SemaphoreType.DMA,
            pltpu.SemaphoreType.DMA((shards * groups,)),
            pltpu.SemaphoreType.DMA((shards * groups,)),
        ],
        compiler_params=pltpu.CompilerParams(collective_id=2, has_side_effects=True),
        name="deliver",
    )(block)


def halves(data):
    high = data.astype(jnp.bfloat16)
    return high, (data - high.astype(jnp.float32)).astype(jnp.bfloat16)


def product(matrix, which, high, low):
    def dot(a, b):
        return jnp.dot(a, b, preferred_element_type=jnp.float32)

    return (
        dot(matrix[which], high) + dot(matrix[which], low) + dot(matrix[which + 1], high)
    )


def spectral_kernel(coef, held, turn, matrix, filt, grad, packed, work):
    shards, groups, _, rows, lanes = held.shape
    length = groups * rows
    total = 2 * length * shards
    part = rows // shards
    for g in range(groups):
        here = pl.ds(g * rows, rows)
        for sig in range(2):
            sums = [jnp.zeros((rows, lanes), jnp.float32) for _ in range(4)]
            for i in range(shards):
                left = held[i, g, 0 if sig == 0 else 3].astype(jnp.float32)
                right = held[i, g, 1 if sig == 0 else 2].astype(jnp.float32)
                value = left * right
                for k in range(4):
                    sums[k] = sums[k] + value * coef[k, i]
            for e in range(2):
                real, imag = sums[2 * e], sums[2 * e + 1]
                cos, sin = turn[e, 0, here], turn[e, 1, here]
                at = (sig * 2 + e) * 2 * lanes
                work[here, at : at + lanes] = real * cos + imag * sin
                work[here, at + lanes : at + 2 * lanes] = imag * cos - real * sin
    span = 2 * lanes
    for e in range(2):
        spectra = []
        for sig in range(2):
            at = (sig * 2 + e) * span
            high, low = halves(work[:, at : at + span])
            by_cos = product(matrix, 0, high, low)
            by_sin = product(matrix, 2, high, low)
            spectra.append(by_cos[:, :lanes] + by_sin[:, lanes:])
            spectra.append(by_cos[:, lanes:] - by_sin[:, :lanes])
        sr, si, cr, ci = spectra
        fr, fi = filt[0, 0, e], filt[1, 0, e]
        grad[0, 0, e] = (sr * cr + si * ci) * (1.0 / total)
        grad[1, 0, e] = (sr * ci - si * cr) * (1.0 / total)
        real = (sr * fr - si * fi) - (fr * ci - fi * cr)
        imag = (sr * fi + si * fr) + (fr * cr + fi * ci)
        high, low = halves(jnp.concatenate([real, imag], axis=1))
        by_cos = product(matrix, 0, high, low)
        by_sin = product(matrix, 2, high, low)
        real = by_cos[:, :lanes] - by_sin[:, lanes:]
        imag = by_cos[:, lanes:] + by_sin[:, :lanes]
        cos, sin = turn[e, 0] * (1.0 / total), turn[e, 1] * (1.0 / total)
        done = (real * cos - imag * sin, real * sin + imag * cos)
        for p in range(2):
            for k in range(shards):
                for g in range(groups):
                    at = g * rows + k * part
                    packed[k, e, p, g * part : (g + 1) * part] = done[p][at : at + part]


def spectral(coef, held, turn, matrix, filt):
    shards, groups, _, rows, width = held.shape
    lanes = 128
    length = groups * rows
    part = length // shards
    filt_block = pl.BlockSpec((2, 1, 2, length, lanes), lambda n: (0, 0, 0, 0, n))
    return pl.pallas_call(
        spectral_kernel,
        grid=(width // lanes,),
        out_shape=(
            jax.ShapeDtypeStruct(filt.shape, jnp.float32),
            jax.ShapeDtypeStruct((shards, 2, 2, part, width), jnp.float32),
        ),
        in_specs=[
            pl.BlockSpec(memory_space=pltpu.SMEM),
            pl.BlockSpec((shards, groups, 4, rows, lanes), lambda n: (0, 0, 0, 0, n)),
            pl.BlockSpec((2, 2, length, lanes), lambda n: (0, 0, 0, 0)),
            pl.BlockSpec((4, length, length), lambda n: (0, 0, 0)),
            filt_block,
        ],
        out_specs=(
            filt_block,
            pl.BlockSpec((shards, 2, 2, part, lanes), lambda n: (0, 0, 0, 0, n)),
        ),
        scratch_shapes=[pltpu.VMEM((length, 8 * lanes), jnp.float32)],
        compiler_params=pltpu.CompilerParams(vmem_limit_bytes=60 * 1024 * 1024),
        name="spectral",
    )(coef, held, turn, matrix, filt)


def rotate(value, numerator, denominator):
    numerator = numerator % denominator
    real, imag = value
    if numerator == 0:
        return value
    if 4 * numerator == denominator:
        return (-imag, real)
    angle = 2.0 * math.pi * numerator / denominator
    cos, sin = math.cos(angle), math.sin(angle)
    return (real * cos - imag * sin, real * sin + imag * cos)


def butterflies(values):
    count = len(values)
    if count == 1:
        return values
    even, odd = butterflies(values[0::2]), butterflies(values[1::2])
    out = [None] * count
    for k in range(count // 2):
        turned = rotate(odd[k], k, count)
        out[k] = (even[k][0] + turned[0], even[k][1] + turned[1])
        out[k + count // 2] = (even[k][0] - turned[0], even[k][1] - turned[1])
    return out


def finish_kernel(pieces, gates, result):
    shards, groups, _, part, width = gates.shape
    bits = shards.bit_length() - 1
    for g in range(groups):
        rows = slice(g * part, (g + 1) * part)
        ladders = []
        for e in range(2):
            order = [mirrored(q, bits) for q in range(shards)]
            ladders.append(
                butterflies([(pieces[r, e, 0, rows], pieces[r, e, 1, rows]) for r in order])
            )
        for i in range(shards):
            odd = rotate(ladders[1][i], i, 2 * shards)
            conv = ladders[0][i][0] + odd[0]
            back = ladders[0][i][1] + odd[1]
            value = gates[i, g, 0].astype(jnp.float32)
            gate_in = gates[i, g, 1].astype(jnp.float32)
            gate_out = gates[i, g, 2].astype(jnp.float32)
            incoming = gates[i, g, 3].astype(jnp.float32)
            result[i, g, 0] = (gate_out * conv).astype(jnp.bfloat16)
            result[i, g, 1] = (back * gate_in).astype(jnp.bfloat16)
            result[i, g, 2] = (back * value).astype(jnp.bfloat16)
            result[i, g, 3] = (incoming * conv).astype(jnp.bfloat16)


def finish(pieces, gates):
    shards, groups, _, part, width = gates.shape
    lanes = 128
    gates_block = pl.BlockSpec((shards, groups, 4, part, lanes), lambda n: (0, 0, 0, 0, n))
    return pl.pallas_call(
        finish_kernel,
        grid=(width // lanes,),
        out_shape=jax.ShapeDtypeStruct(gates.shape, jnp.bfloat16),
        in_specs=[
            pl.BlockSpec((shards, 2, 2, groups * part, lanes), lambda n: (0, 0, 0, 0, n)),
            gates_block,
        ],
        out_specs=gates_block,
        name="finish",
    )(pieces, gates)


def transform_matrix(length):
    counter = np.arange(length)
    angle = 2.0 * math.pi * (np.outer(counter, counter) % length) / length
    out = []
    for table in (np.cos(angle), np.sin(angle)):
        high = table.astype(jnp.bfloat16)
        out += [high, (table - high.astype(np.float64)).astype(jnp.bfloat16)]
    return jnp.asarray(np.stack(out))


def on_device(shards, groups, values_in, gate_in, gate_out, cotangent, filter_spectra):
    rows = values_in.shape[0]
    length = rows * groups
    total = 2 * length * shards
    index = lax.axis_index("seq")
    residue = 2 * mirrored(index, shards.bit_length() - 1) + jnp.arange(2, dtype=jnp.int32)
    shard = jnp.arange(shards, dtype=jnp.int32)
    angle = (2.0 * math.pi / (2 * shards)) * (
        residue[:, None] * shard[None, :] % (2 * shards)
    ).astype(jnp.float32)
    coef = jnp.stack([jnp.cos(angle), -jnp.sin(angle)], axis=1).reshape(4, shards)
    position = jnp.arange(length, dtype=jnp.int32)
    angle = (2.0 * math.pi / total) * (residue[:, None] * position[None, :] % total).astype(
        jnp.float32
    )
    turn = jnp.stack([jnp.cos(angle), jnp.sin(angle)], axis=1)
    turn = jnp.broadcast_to(turn[..., None], (2, 2, length, 128))

    held = gather((values_in, gate_in, gate_out, cotangent), shards, groups)
    grad_filter, packed = spectral(coef, held, turn, transform_matrix(length), filter_spectra)
    part = rows // shards
    gates = lax.dynamic_slice_in_dim(held, index * part, part, axis=3)
    result = deliver(finish(trade(packed), gates))
    outs = [
        result[:, :, a].transpose(0, 2, 1, 3).reshape(rows, values_in.shape[1]) for a in range(4)
    ]
    return (outs[0], outs[1], outs[2], outs[3], grad_filter)


def solution(mesh):
    tokens = P(("seq", "chan"), None)
    spectrum = P(None, "seq", None, None, "chan")
    return jax.shard_map(
        functools.partial(on_device, mesh.shape["seq"], mesh.shape["chan"]),
        mesh=mesh,
        in_specs=(tokens, tokens, tokens, tokens, spectrum),
        out_specs=(tokens, tokens, tokens, tokens, spectrum),
        check_vma=False,
    )
```

time: 352 us -> 171 us (0.49); the launches traced: 346 us -> 171 us
  Pallas kernels: 0 us -> 161 us
  waiting for transfers between devices: 104 us -> 0 us
  blocking collectives: 103 us -> 0 us
  matrix products: 60.1 us -> 0 us
  starting transfers between devices: 32.3 us -> 0 us
  local copies, waits for them, and re-layouts: 35.3 us -> 8.54 us
  other arithmetic: 9.93 us -> 0.94 us
    pallas_call x0 -> x5, Pallas kernels: none -> 161 us  [the longest x1 81.1 us: gather(): pl.pallas_call(functools.partial(gather_kernel, shards, groups), out_shap...]
    all_to_all x8 -> x0, waiting for transfers between devices: 104 us -> none  [the longest x1 46.9 us: forward_rows_spread(): lax.all_to_all(mixed, 'seq', split_axis=3, concat_axis=4, tiled=True)]
    all_to_all x4 -> x0, blocking collectives: 103 us -> none  [the longest x1 52.6 us: forward_rows_spread(): lax.all_to_all(block[:, :, :, None], 'seq', split_axis=4, concat_axis=3,...]
    dot_general x24 -> x0, matrix products: 60.1 us -> none  [the longest x8 21.7 us: first_pass(): return jnp.einsum('kt,...tad->...kad', matrix, data, precision=highest)]
    all_to_all x8 -> x0, starting transfers between devices: 32.3 us -> none  [the longest x1 6.35 us: on_device(): lax.all_to_all(values_in, 'chan', split_axis=1, concat_axis=0, tiled=True)]
    unnamed x34 -> x4, local copies, waits for them, and re-layouts: 11.1 us -> 2.96 us
    another operation x2 -> x0, local copies, waits for them, and re-layouts: 5.27 us -> none  [mix_shards(): return jnp.stack([mixed_real, mixed_imag], axis=1)]
    slice x8 -> x0, local copies, waits for them, and re-layouts: 5.12 us -> none  [the longest x1 1.68 us: on_device(): filt_real = filter_spectra[0, 0]]
  transfers between devices with their start and end apart: 8 -> 0, of which waited for: 8 -> 0; matrix products, arithmetic and copies ran while one was open for 4% -> 0% of each run, Pallas kernels for 0% -> 0%
where the time goes in v1:
time: 171 us
  Pallas kernels  161 us (94%)
  local copies, waits for them, and re-layouts  8.54 us (5%)
    pallas_call x1, Pallas kernels, gather(): pl.pallas_call(functools.partial(gather_kernel, shards, groups), out_shap...  81.1 us
    pallas_call x1, Pallas kernels, deliver(): pl.pallas_call(functools.partial(deliver_kernel, shards, groups), out_sha...  30.3 us
    pallas_call x1, Pallas kernels, trade(): pl.pallas_call(functools.partial(trade_kernel, shards), out_shape=jax.Sha...  28.4 us
    pallas_call x1, Pallas kernels, spectral(): pl.pallas_call(spectral_kernel, grid=(width // lanes,), out_shape=(jax.Sh...  17.9 us

profile of v1, /device:TPU:0, one launch (start us, length us, event | category | flops | bytes accessed | tf_op | source)
XLA Modules:
  0.0 171.0 jit_solution(8695258029862839166)
XLA Ops:
  0.7 0.2 fusion.4
  0.9 1.4 broadcast_in_dim.2.turn
  2.3 0.1 fusion.8
  2.4 0.6 pad_maximum_fusion.1
  3.0 81.1 %gather.1.held = bf16[8,4,4,128,256]{4,3,2,1,0:T(8,128)(2,1)} custom-call(bf16[128,1024]{1,0:T(8,128)(2,1)} %refs_0_.1, bf16[128,1024]{1,0:T(8,128)(2,1)} %refs_1_.1, bf16[128,1024]{1,0:T(8,128)(2,1)} %refs_2_.1, bf16[128,1024]{1,0:T(8,128)(2,1)} %refs_3_.1), custom_call_target="tpu_custom_call" | custom-call | tf_op jit(solution)/shard_map/gather/pallas_call | solution.py:119
  84.1 17.9 %spectral.1 = (f32[2,1,2,512,256]{4,3,2,1,0:T(8,128)}, f32[8,2,2,64,256]{4,3,2,1,0:T(8,128)}) custom-call(f32[4,8]{1,0:T(4,128)} %bitcast.37, bf16[8,4,4,128,256]{4,3,2,1,0:T(8,128)(2,1)} %gather.1.held, f32[2,2,512,128]{3,2,1,0:T(8,128)} %broadcast_in_dim.2.turn, bf16[4,512,512]{2,1,0:T(8,128)(2,1)} %constant.50.clone.matrix, f32[2,1,2,512,256]{4,3,2,1,0:T(8,128)} %filt.1), custom_call_target="tpu_custom_call" | custom-call | tf_op jit(solution)/shard_map/spectral/pallas_call | solution.py:303
  102.0 28.4 %trade.1.pieces = f32[8,2,2,64,256]{4,3,2,1,0:T(8,128)} custom-call(f32[8,2,2,64,256]{4,3,2,1,0:T(8,128)} %get-tuple-element.7.source), custom_call_target="tpu_custom_call" | custom-call | tf_op jit(solution)/shard_map/trade/pallas_call | solution.py:173
  130.5 2.3 %constant_dynamic-slice_fusion.gates = bf16[8,4,4,16,256]{4,3,2,1,0:T(8,128)(2,1)} fusion(bf16[8,4,4,128,256]{4,3,2,1,0:T(8,128)(2,1)} %gather.1.held, s32[]{:T(128)S(6)} %select_n.40), kind=kLoop, calls=%fused_computation.23 | loop fusion | bytes 2097156 | tf_op jit(solution)/shard_map/dynamic_slice | solution.py:425
  132.8 3.0 %finish.1.source = bf16[8,4,4,16,256]{4,3,2,1,0:T(8,128)(2,1)} custom-call(f32[8,2,2,64,256]{4,3,2,1,0:T(8,128)} %trade.1.pieces, bf16[8,4,4,16,256]{4,3,2,1,0:T(8,128)(2,1)} %constant_dynamic-slice_fusion.gates), custom_call_target="tpu_custom_call" | custom-call | tf_op jit(solution)/shard_map/finish/pallas_call | solution.py:381
  135.8 30.3 %deliver.1 = bf16[8,4,4,16,256]{4,3,2,1,0:T(8,128)(2,1)} custom-call(bf16[8,4,4,16,256]{4,3,2,1,0:T(8,128)(2,1)} %finish.1.source), custom_call_target="tpu_custom_call" | custom-call | tf_op jit(solution)/shard_map/deliver/pallas_call | solution.py:217
  166.1 1.3 slice_bitcast_fusion
  167.4 0.1 copy.11
  167.6 0.7 copy.15
  168.3 0.1 copy.12
  168.4 0.7 copy.16
  169.2 0.1 copy.13
  169.3 0.7 copy.17
  170.1 0.1 copy.14
  170.2 0.7 copy.18
  (2 shorter events, 0.0 us)

commit v2 on v1

v2 whole, which is shorter than its diff:
```python
import functools
import math

import jax
import jax.numpy as jnp
import numpy as np
from jax import lax
from jax.experimental import pallas as pl
from jax.experimental.pallas import tpu as pltpu
from jax.sharding import PartitionSpec as P

MESH = pl.DeviceIdType.MESH
ANY = pl.BlockSpec(memory_space=pl.ANY)
WHOLE = pl.BlockSpec(memory_space=pltpu.VMEM)


def mirrored(number, bits):
    out = 0
    for place in range(bits):
        out = out + ((number >> place) & 1) * (1 << (bits - 1 - place))
    return out


def meet(peers):
    barrier = pltpu.get_barrier_semaphore()
    for peer in peers:
        pl.semaphore_signal(barrier, inc=1, device_id=peer, device_id_type=MESH)
    pl.semaphore_wait(barrier, len(peers))


def gather_kernel(shards, groups, *refs):
    inputs, filt, held, other = refs[:4], refs[4], refs[5], refs[6]
    own_sem, z_send, z_recv, s_send, s_recv, f_send, f_recv = refs[7:]
    s, c = lax.axis_index("seq"), lax.axis_index("chan")
    half = s % 2
    pair = s // 2
    width = inputs[0].shape[1] // groups
    lanes = width // 2
    bits = shards.bit_length() - 1
    near = [(d, e) for d in range(groups) for e in range(2) if d or e]
    meet([(s ^ e, c ^ d) for d, e in near] + [(s ^ (1 << b), c) for b in range(1, bits)])

    def columns(group, side):
        return pl.ds(pl.multiple_of(group * width + side * lanes, lanes), lanes)

    def cross(d, e, a, landing):
        at = (d * 2 + e) * 4 + a
        return pltpu.make_async_remote_copy(
            src_ref=inputs[a].at[:, columns(c ^ d, half ^ e)],
            dst_ref=held.at[s ^ e, c ^ d, a] if landing else held.at[s, c, a],
            send_sem=z_send.at[at],
            recv_sem=z_recv.at[at],
            device_id=(s ^ e, c ^ d),
            device_id_type=MESH,
        )

    for d, e in near:
        for a in range(4):
            cross(d, e, a, False).start()
    own = [
        pltpu.make_async_copy(inputs[a].at[:, columns(c, half)], held.at[s, c, a], own_sem.at[a])
        for a in range(4)
    ]
    for copy in own:
        copy.start()
    swap = pltpu.make_async_remote_copy(
        src_ref=filt.at[:, :, :, :, columns(0, half ^ 1)],
        dst_ref=other,
        send_sem=f_send,
        recv_sem=f_recv,
        device_id=(s ^ 1, c),
        device_id_type=MESH,
    )

    def piece(d, owner, slot, partner):
        place = held.at[pl.ds(owner * 2, 2), c ^ d]
        return pltpu.make_async_remote_copy(
            src_ref=place,
            dst_ref=place,
            send_sem=s_send.at[d * (shards // 2) + slot],
            recv_sem=s_recv.at[d * (shards // 2) + slot],
            device_id=(partner * 2 + half, c),
            device_id_type=MESH,
        )

    far = list(range(bits - 1))
    sent, landed = [], []
    for tick in range(groups + bits):
        for d in range(groups):
            order = far if d % 2 == 0 else far[::-1]
            depth = tick - d
            for mask in range(shards // 2):
                if bin(mask).count("1") != depth:
                    continue
                last = max([order.index(b) for b in far if mask >> b & 1], default=-1)
                later = order[last + 1 :]
                if not later:
                    landed.append((d, mask))
                    continue
                if mask:
                    piece(d, pair ^ mask, mask, pair).wait_recv()
                else:
                    for e in range(2):
                        for a in range(4):
                            if d or e:
                                cross(d, e, a, True).wait_recv()
                            else:
                                own[a].wait()
                for b in later:
                    copy = piece(d, pair ^ mask, mask ^ (1 << b), pair ^ (1 << b))
                    copy.start()
                    sent.append(copy)
        if tick == 0:
            swap.start()
    for d, mask in landed:
        piece(d, pair ^ mask, mask, pair).wait_recv()
    swap.wait_recv()
    for d, e in near:
        for a in range(4):
            cross(d, e, a, False).wait_send()
    for copy in sent:
        copy.wait_send()
    swap.wait_send()


def gather(inputs, filt, shards, groups):
    rows, channels = inputs[0].shape
    lanes = channels // groups // 2
    return pl.pallas_call(
        functools.partial(gather_kernel, shards, groups),
        out_shape=(
            jax.ShapeDtypeStruct((shards, groups, 4, rows, lanes), inputs[0].dtype),
            jax.ShapeDtypeStruct(filt.shape[:-1] + (lanes,), filt.dtype),
        ),
        in_specs=[WHOLE] * 4 + [ANY],
        out_specs=(ANY, ANY),
        scratch_shapes=[
            pltpu.SemaphoreType.DMA((4,)),
            pltpu.SemaphoreType.DMA((groups * 8,)),
            pltpu.SemaphoreType.DMA((groups * 8,)),
            pltpu.SemaphoreType.DMA((groups * shards // 2,)),
            pltpu.SemaphoreType.DMA((groups * shards // 2,)),
            pltpu.SemaphoreType.DMA,
            pltpu.SemaphoreType.DMA,
        ],
        compiler_params=pltpu.CompilerParams(collective_id=0, has_side_effects=True),
        name="gather",
    )(*inputs, filt)


def trade_kernel(shards, source, grad, target, other, own_sem, send_sem, recv_sem):
    s, c = lax.axis_index("seq"), lax.axis_index("chan")
    pairs = shards // 2
    pair, half = s // 2, s % 2
    meet([((pair ^ j) * 2 + half, c) for j in range(1, pairs)] + [(s ^ 1, c)])

    def transfer(j, landing):
        return pltpu.make_async_remote_copy(
            src_ref=source.at[pair ^ j],
            dst_ref=target.at[pair ^ j] if landing else target.at[pair],
            send_sem=send_sem.at[j],
            recv_sem=recv_sem.at[j],
            device_id=((pair ^ j) * 2 + half, c),
            device_id_type=MESH,
        )

    swap = pltpu.make_async_remote_copy(
        src_ref=grad,
        dst_ref=other,
        send_sem=send_sem.at[0],
        recv_sem=recv_sem.at[0],
        device_id=(s ^ 1, c),
        device_id_type=MESH,
    )
    for j in range(pairs - 1, 0, -1):
        transfer(j, False).start()
    swap.start()
    own = pltpu.make_async_copy(source.at[pair], target.at[pair], own_sem)
    own.start()
    own.wait()
    swap.wait_recv()
    for j in range(1, pairs):
        transfer(j, True).wait_recv()
    for j in range(1, pairs):
        transfer(j, False).wait_send()
    swap.wait_send()


def trade(block, grad):
    pairs = block.shape[0]
    return pl.pallas_call(
        functools.partial(trade_kernel, 2 * pairs),
        out_shape=(
            jax.ShapeDtypeStruct(block.shape, block.dtype),
            jax.ShapeDtypeStruct(grad.shape, grad.dtype),
        ),
        in_specs=[WHOLE, ANY],
        out_specs=(ANY, ANY),
        scratch_shapes=[
            pltpu.SemaphoreType.DMA,
            pltpu.SemaphoreType.DMA((pairs,)),
            pltpu.SemaphoreType.DMA((pairs,)),
        ],
        compiler_params=pltpu.CompilerParams(collective_id=1, has_side_effects=True),
        name="trade",
    )(block, grad)


def deliver_kernel(shards, groups, source, target, own_sem, send_sem, recv_sem):
    s, c = lax.axis_index("seq"), lax.axis_index("chan")
    peers = [(j, d) for d in range(groups - 1, -1, -1) for j in range(shards) if j or d]
    meet([(s ^ j, c ^ d) for j, d in peers])

    def transfer(j, d, landing):
        to_s, to_c = (s ^ j, c ^ d) if landing else (s, c)
        return pltpu.make_async_remote_copy(
            src_ref=source.at[s ^ j, c ^ d],
            dst_ref=target.at[to_s, to_c],
            send_sem=send_sem.at[d * shards + j],
            recv_sem=recv_sem.at[d * shards + j],
            device_id=(s ^ j, c ^ d),
            device_id_type=MESH,
        )

    for j, d in peers:
        transfer(j, d, False).start()
    own = pltpu.make_async_copy(source.at[s, c], target.at[s, c], own_sem)
    own.start()
    own.wait()
    for j, d in peers:
        transfer(j, d, True).wait_recv()
    for j, d in peers:
        transfer(j, d, False).wait_send()


def deliver(block):
    shards, groups = block.shape[:2]
    return pl.pallas_call(
        functools.partial(deliver_kernel, shards, groups),
        out_shape=jax.ShapeDtypeStruct(block.shape, block.dtype),
        in_specs=[WHOLE],
        out_specs=ANY,
        scratch_shapes=[
            pltpu.SemaphoreType.DMA,
            pltpu.SemaphoreType.DMA((shards * groups,)),
            pltpu.SemaphoreType.DMA((shards * groups,)),
        ],
        compiler_params=pltpu.CompilerParams(collective_id=2, has_side_effects=True),
        name="deliver",
    )(block)


def halves(data):
    high = data.astype(jnp.bfloat16)
    return high, (data - high.astype(jnp.float32)).astype(jnp.bfloat16)


def product(matrix, which, high, low):
    def dot(a, b):
        return jnp.dot(a, b, preferred_element_type=jnp.float32)

    return (
        dot(matrix[which], high) + dot(matrix[which], low) + dot(matrix[which + 1], high)
    )


def spectral_kernel(side, coef, held, turn, matrix, filt, other, grad, away, packed, work):
    shards, groups, _, rows, lanes = held.shape
    length = groups * rows
    total = 2 * length * shards
    part = rows * 2 // shards
    step = pl.program_id(0)
    sign = (1 - 2 * side[0]).astype(jnp.float32)

    for g in range(groups):
        here = pl.ds(g * rows, rows)
        for sig in range(2):
            sums = [[None, None], [None, None]]
            for i in range(shards):
                left = held[i, g, 0 if sig == 0 else 3].astype(jnp.float32)
                right = held[i, g, 1 if sig == 0 else 2].astype(jnp.float32)
                value = left * right
                for p in range(2):
                    term = value * coef[step * 2 + p, i]
                    sums[p][i % 2] = term if i < 2 else sums[p][i % 2] + term
            for w in range(2):
                real, imag = (
                    sums[p][0] + sums[p][1] if w == 0 else sums[p][0] - sums[p][1]
                    for p in range(2)
                )
                cos, sin = turn[w, 0, 0, here], turn[w, 0, 1, here]
                at = (w * 2 + sig) * 2 * lanes
                work[here, at : at + lanes] = real * cos + imag * sin
                work[here, at + lanes : at + 2 * lanes] = imag * cos - real * sin
    span = 2 * lanes
    found = []
    for w in range(2):
        spectra = []
        for sig in range(2):
            at = (w * 2 + sig) * span
            high, low = halves(work[:, at : at + span])
            by_cos = product(matrix, 0, high, low)
            by_sin = product(matrix, 2, high, low)
            spectra.append(by_cos[:, :lanes] + by_sin[:, lanes:])
            spectra.append(by_cos[:, lanes:] - by_sin[:, :lanes])
        sr, si, cr, ci = spectra
        spectrum, slope = ((filt, grad), (other, away))[w]
        fr, fi = spectrum[0, 0, 0], spectrum[1, 0, 0]
        slope[0, 0, 0] = (sr * cr + si * ci) * (1.0 / total)
        slope[1, 0, 0] = (sr * ci - si * cr) * (1.0 / total)
        real = (sr * fr - si * fi) - (fr * ci - fi * cr)
        imag = (sr * fi + si * fr) + (fr * cr + fi * ci)
        high, low = halves(jnp.concatenate([real, imag], axis=1))
        by_cos = product(matrix, 0, high, low)
        by_sin = product(matrix, 2, high, low)
        real = by_cos[:, :lanes] - by_sin[:, lanes:]
        imag = by_cos[:, lanes:] + by_sin[:, :lanes]
        cos, sin = turn[w, 0, 0] * (1.0 / total), turn[w, 0, 1] * (1.0 / total)
        found.append((real * cos - imag * sin, real * sin + imag * cos))
    for p in range(2):
        done = (found[0][p] + found[1][p], (found[0][p] - found[1][p]) * sign)
        for v in range(2):
            for k in range(shards // 2):
                for g in range(groups):
                    at = g * rows + k * part
                    packed[k, v, 0, p, g * part : (g + 1) * part] = done[v][at : at + part]


def spectral(side, coef, held, turn, matrix, filt, other):
    shards, groups, _, rows, lanes = held.shape
    length = groups * rows
    pairs = shards // 2
    part = length // pairs
    half_block = pl.BlockSpec((2, 1, 1, length, lanes), lambda n, side: (0, 0, n, 0, 0))
    return pl.pallas_call(
        spectral_kernel,
        grid_spec=pltpu.PrefetchScalarGridSpec(
            num_scalar_prefetch=1,
            grid=(2,),
            in_specs=[
                pl.BlockSpec(memory_space=pltpu.SMEM),
                pl.BlockSpec((shards, groups, 4, rows, lanes), lambda n, side: (0, 0, 0, 0, 0)),
                pl.BlockSpec((2, 1, 2, length, lanes), lambda n, side: (0, n, 0, 0, 0)),
                pl.BlockSpec((4, length, length), lambda n, side: (0, 0, 0)),
                pl.BlockSpec((2, 1, 1, length, lanes), lambda n, side: (0, 0, n, 0, side[0])),
                half_block,
            ],
            out_specs=(
                half_block,
                half_block,
                pl.BlockSpec((pairs, 2, 1, 2, part, lanes), lambda n, side: (0, 0, n, 0, 0, 0)),
            ),
            scratch_shapes=[pltpu.VMEM((length, 8 * lanes), jnp.float32)],
        ),
        out_shape=(
            jax.ShapeDtypeStruct(other.shape, jnp.float32),
            jax.ShapeDtypeStruct(other.shape, jnp.float32),
            jax.ShapeDtypeStruct((pairs, 2, 2, 2, part, lanes), jnp.float32),
        ),
        compiler_params=pltpu.CompilerParams(vmem_limit_bytes=60 * 1024 * 1024),
        name="spectral",
    )(side, coef, held, turn, matrix, filt, other)


def rotate(value, numerator, denominator):
    numerator = numerator % denominator
    real, imag = value
    if numerator == 0:
        return value
    if 4 * numerator == denominator:
        return (-imag, real)
    angle = 2.0 * math.pi * numerator / denominator
    cos, sin = math.cos(angle), math.sin(angle)
    return (real * cos - imag * sin, real * sin + imag * cos)


def butterflies(values):
    count = len(values)
    if count == 1:
        return values
    even, odd = butterflies(values[0::2]), butterflies(values[1::2])
    out = [None] * count
    for k in range(count // 2):
        turned = rotate(odd[k], k, count)
        out[k] = (even[k][0] + turned[0], even[k][1] + turned[1])
        out[k + count // 2] = (even[k][0] - turned[0], even[k][1] - turned[1])
    return out


def finish_kernel(pieces, gates, result):
    shards, _, _, part, lanes = gates.shape
    pairs = shards // 2
    bits = pairs.bit_length() - 1
    ladders = {}
    for e in range(2):
        for v in range(2):
            terms = []
            for q in range(pairs):
                k = mirrored(q, bits)
                terms.append(rotate((pieces[k, v, e, 0], pieces[k, v, e, 1]), q * v, shards))
            ladders[e, v] = butterflies(terms)
    for i in range(shards):
        plain = ladders[0, i % 2][i // 2]
        odd = rotate(ladders[1, i % 2][i // 2], i, 2 * shards)
        conv = plain[0] + odd[0]
        back = plain[1] + odd[1]
        value = gates[i, 0, 0].astype(jnp.float32)
        gate_in = gates[i, 0, 1].astype(jnp.float32)
        gate_out = gates[i, 0, 2].astype(jnp.float32)
        incoming = gates[i, 0, 3].astype(jnp.float32)
        result[i, 0, 0] = (gate_out * conv).astype(jnp.bfloat16)
        result[i, 0, 1] = (back * gate_in).astype(jnp.bfloat16)
        result[i, 0, 2] = (back * value).astype(jnp.bfloat16)
        result[i, 0, 3] = (incoming * conv).astype(jnp.bfloat16)


def finish(pieces, gates):
    shards, groups, _, part, lanes = gates.shape
    gates_block = pl.BlockSpec((shards, 1, 4, part, lanes), lambda n: (0, n, 0, 0, 0))
    return pl.pallas_call(
        finish_kernel,
        grid=(groups,),
        out_shape=jax.ShapeDtypeStruct(gates.shape, jnp.bfloat16),
        in_specs=[
            pl.BlockSpec((shards // 2, 2, 2, 2, part, lanes), lambda n: (0, 0, 0, 0, n, 0)),
            gates_block,
        ],
        out_specs=gates_block,
        name="finish",
    )(pieces, gates)


def transform_matrix(length):
    counter = np.arange(length)
    angle = 2.0 * math.pi * (np.outer(counter, counter) % length) / length
    out = []
    for table in (np.cos(angle), np.sin(angle)):
        high = table.astype(jnp.bfloat16)
        out += [high, (table - high.astype(np.float64)).astype(jnp.bfloat16)]
    return jnp.asarray(np.stack(out))


def on_device(shards, groups, values_in, gate_in, gate_out, cotangent, filter_spectra):
    rows = values_in.shape[0]
    length = rows * groups
    total = 2 * length * shards
    index = lax.axis_index("seq")
    side = index % 2
    own = 2 * mirrored(index, shards.bit_length() - 1) + jnp.arange(2, dtype=jnp.int32)
    shard = jnp.arange(shards, dtype=jnp.int32)
    angle = (2.0 * math.pi / (2 * shards)) * (own[:, None] * shard[None, :] % (2 * shards)).astype(
        jnp.float32
    )
    coef = jnp.stack([jnp.cos(angle), -jnp.sin(angle)], axis=1).reshape(4, shards)
    position = jnp.arange(length, dtype=jnp.int32)
    residue = jnp.stack([own, (own + shards) % (2 * shards)])
    angle = (2.0 * math.pi / total) * (residue[..., None] * position % total).astype(jnp.float32)
    turn = jnp.stack([jnp.cos(angle), jnp.sin(angle)], axis=2)
    turn = jnp.broadcast_to(turn[..., None], (2, 2, 2, length, 128))

    held, other = gather(
        (values_in, gate_in, gate_out, cotangent), filter_spectra, shards, groups
    )
    mine, away, packed = spectral(
        side[None], coef, held, turn, transform_matrix(length), filter_spectra, other
    )
    pieces, theirs = trade(packed, away)
    part = rows * 2 // shards
    gates = lax.dynamic_slice_in_dim(held, index // 2 * part, part, axis=3)
    result = deliver(finish(pieces, gates))
    result = result.reshape((shards // 2, 2) + result.shape[1:])
    outs = [
        result[:, :, :, a].transpose(0, 3, 2, 1, 4).reshape(rows, values_in.shape[1])
        for a in range(4)
    ]
    grad_filter = jnp.concatenate(
        [jnp.where(side == 0, mine, theirs), jnp.where(side == 0, theirs, mine)], axis=-1
    )
    return (outs[0], outs[1], outs[2], outs[3], grad_filter)


def solution(mesh):
    tokens = P(("seq", "chan"), None)
    spectrum = P(None, "seq", None, None, "chan")
    return jax.shard_map(
        functools.partial(on_device, mesh.shape["seq"], mesh.shape["chan"]),
        mesh=mesh,
        in_specs=(tokens, tokens, tokens, tokens, spectrum),
        out_specs=(tokens, tokens, tokens, tokens, spectrum),
        check_vma=False,
    )
```

time: 171 us -> 153 us (0.89)
  Pallas kernels: 161 us -> 139 us
  other arithmetic: 0.94 us -> 2.69 us
    pallas_call x1, Pallas kernels: 81.1 us -> 60.8 us  [gather(): pl.pallas_call(functools.partial(gather_kernel, shards, groups), out_shap...]
    reshape x0 -> x4, local copies, waits for them, and re-layouts: none -> 3.49 us  [on_device(): result[:, :, :, a].transpose(0, 3, 2, 1, 4)]
    unnamed x4, local copies, waits for them, and re-layouts: 2.96 us -> 0.01 us
where the time goes in v2:
time: 153 us
  Pallas kernels  139 us (91%)
  local copies, waits for them, and re-layouts  10.1 us (7%)
  other arithmetic  2.69 us (2%)
    pallas_call x1, Pallas kernels, gather(): pl.pallas_call(functools.partial(gather_kernel, shards, groups), out_shap...  60.8 us
    pallas_call x1, Pallas kernels, deliver(): pl.pallas_call(functools.partial(deliver_kernel, shards, groups), out_sha...  29.8 us
    pallas_call x1, Pallas kernels, trade(): pl.pallas_call(functools.partial(trade_kernel, 2 * pairs), out_shape=(jax...  27.1 us
    pallas_call x1, Pallas kernels, spectral(): pl.pallas_call(spectral_kernel, grid_spec=pltpu.PrefetchScalarGridSpec(nu...  17.3 us
    pallas_call x1, Pallas kernels, finish(): pl.pallas_call(finish_kernel, grid=(groups,), out_shape=jax.ShapeDtypeStr...  3.97 us
    reshape x4, local copies, waits for them, and re-layouts, on_device(): result[:, :, :, a].transpose(0, 3, 2, 1, 4)  3.49 us

profile of v2, /device:TPU:0, one launch (start us, length us, event | category | flops | bytes accessed | tf_op | source)
XLA Modules:
  0.0 152.6 jit_solution(10794621809847809820)
XLA Ops:
  0.7 0.1 fusion.9
  0.8 0.6 pad_maximum_fusion.2
  1.4 0.3 fusion.4
  1.8 1.9 %broadcast_in_dim.5.turn = f32[2,2,2,512,128]{4,3,2,1,0:T(8,128)} broadcast(f32[2,2,2,512]{3,2,1,0:T(2,128)S(1)} %pad_maximum_fusion.1), dimensions={0,1,2,3} | broadcast | bytes 2113536 | tf_op jit(solution)/shard_map/broadcast_in_dim | solution.py:459
  3.7 60.8 %gather.1 = (bf16[8,4,4,128,128]{4,3,2,1,0:T(8,128)(2,1)}, f32[2,1,2,512,128]{4,3,2,1,0:T(8,128)}) custom-call(bf16[128,1024]{1,0:T(8,128)(2,1)} %refs_0_.1, bf16[128,1024]{1,0:T(8,128)(2,1)} %refs_1_.1, bf16[128,1024]{1,0:T(8,128)(2,1)} %refs_2_.1, bf16[128,1024]{1,0:T(8,128)(2,1)} %refs_3_.1, f32[2,1,2,512,256]{4,3,2,1,0:T(8,128)} %filt.1), custom_call_target="tpu_custom_call" | custom-call | tf_op jit(solution)/shard_map/gather/pallas_call | solution.py:129
  64.6 17.3 %spectral.1 = (f32[2,1,2,512,128]{4,3,2,1,0:T(8,128)}, f32[2,1,2,512,128]{4,3,2,1,0:T(8,128)}, f32[4,2,2,2,128,128]{5,4,3,2,1,0:T(8,128)}) custom-call(s32[1]{0:T(128)} %bitcast.side, f32[4,8]{1,0:T(4,128)} %bitcast.20, bf16[8,4,4,128,128]{4,3,2,1,0:T(8,128)(2,1)} %get-tuple-element.12.held, f32[2,2,2,512,128]{4,3,2,1,0:T(8,128)} %broadcast_in_dim.5.turn, ...), custom_call_target="tpu_custom_call" | custom-call | tf_op jit(solution)/shard_map/spectral/pallas_call | solution.py:335
  81.9 2.3 %constant_dynamic-slice_fusion.gates = bf16[8,4,4,32,128]{4,3,2,1,0:T(8,128)(2,1)} fusion(bf16[8,4,4,128,128]{4,3,2,1,0:T(8,128)(2,1)} %get-tuple-element.12.held, s32[]{:T(128)S(6)} %select_n.78), kind=kLoop, calls=%fused_computation.32 | loop fusion | bytes 2097156 | tf_op jit(solution)/shard_map/dynamic_slice | solution.py:469
  84.2 27.1 %trade.1 = (f32[4,2,2,2,128,128]{5,4,3,2,1,0:T(8,128)}, f32[2,1,2,512,128]{4,3,2,1,0:T(8,128)}) custom-call(f32[4,2,2,2,128,128]{5,4,3,2,1,0:T(8,128)} %get-tuple-element.14.source, f32[2,1,2,512,128]{4,3,2,1,0:T(8,128)} %get-tuple-element.15.grad), custom_call_target="tpu_custom_call" | custom-call | tf_op jit(solution)/shard_map/trade/pallas_call | solution.py:191
  111.3 4.0 %finish.1.source = bf16[8,4,4,32,128]{4,3,2,1,0:T(8,128)(2,1)} custom-call(f32[4,2,2,2,128,128]{5,4,3,2,1,0:T(8,128)} %get-tuple-element.16.pieces, bf16[8,4,4,32,128]{4,3,2,1,0:T(8,128)(2,1)} %constant_dynamic-slice_fusion.gates), custom_call_target="tpu_custom_call" | custom-call | tf_op jit(solution)/shard_map/finish/pallas_call | solution.py:420
  115.3 29.8 %deliver.1 = bf16[8,4,4,32,128]{4,3,2,1,0:T(8,128)(2,1)} custom-call(bf16[8,4,4,32,128]{4,3,2,1,0:T(8,128)(2,1)} %finish.1.source), custom_call_target="tpu_custom_call" | custom-call | tf_op jit(solution)/shard_map/deliver/pallas_call | solution.py:238
  145.1 1.3 slice_bitcast_fusion
  146.4 0.0 copy-start
  146.4 0.0 copy-start.1
  146.4 0.3 copy.14
  146.7 0.9 reshape.230
  147.6 0.3 copy.13
  147.8 0.9 reshape.229
  148.7 0.3 copy.12
  149.0 0.9 reshape.228
  149.9 0.3 copy.11
  150.1 0.9 reshape.227
  151.0 0.0 copy-done
  151.0 0.0 copy-done.1
  151.0 0.1 broadcast_select_fusion.1
  151.2 1.5 pad_maximum_fusion
  (4 shorter events, 0.0 us)
Async XLA Ops:
  146.4 4.6 %copy-start = (f32[2,1,2,512,128]{4,3,2,1,0:T(8,128)S(1)}, f32[2,1,2,512,128]{4,3,2,1,0:T(8,128)}, u32[]{:S(2)}) copy-start(f32[2,1,2,512,128]{4,3,2,1,0:T(8,128)} %get-tuple-element.17) | copy-start | bytes 3145732
  146.4 4.6 %copy-start.1 = (f32[2,1,2,512,128]{4,3,2,1,0:T(8,128)S(1)}, f32[2,1,2,512,128]{4,3,2,1,0:T(8,128)}, u32[]{:S(2)}) copy-start(f32[2,1,2,512,128]{4,3,2,1,0:T(8,128)} %get-tuple-element.18) | copy-start | bytes 3145732

commit v3 on v2

--- a/solution.py
+++ b/solution.py
@@ -29,42 +29,32 @@
 
 
 def gather_kernel(shards, groups, *refs):
-    inputs, filt, held, other = refs[:4], refs[4], refs[5], refs[6]
-    own_sem, z_send, z_recv, s_send, s_recv, f_send, f_recv = refs[7:]
+    source, filt, held, other = refs[:4]
+    own_sem, z_send, z_recv, s_send, s_recv, f_send, f_recv = refs[4:]
     s, c = lax.axis_index("seq"), lax.axis_index("chan")
     half = s % 2
     pair = s // 2
-    width = inputs[0].shape[1] // groups
-    lanes = width // 2
+    lanes = source.shape[-1]
     bits = shards.bit_length() - 1
     near = [(d, e) for d in range(groups) for e in range(2) if d or e]
     meet([(s ^ e, c ^ d) for d, e in near] + [(s ^ (1 << b), c) for b in range(1, bits)])
 
-    def columns(group, side):
-        return pl.ds(pl.multiple_of(group * width + side * lanes, lanes), lanes)
-
-    def cross(d, e, a, landing):
-        at = (d * 2 + e) * 4 + a
+    def cross(d, e, landing):
         return pltpu.make_async_remote_copy(
-            src_ref=inputs[a].at[:, columns(c ^ d, half ^ e)],
-            dst_ref=held.at[s ^ e, c ^ d, a] if landing else held.at[s, c, a],
-            send_sem=z_send.at[at],
-            recv_sem=z_recv.at[at],
+            src_ref=source.at[c ^ d, half ^ e],
+            dst_ref=held.at[s ^ e, c ^ d] if landing else held.at[s, c],
+            send_sem=z_send.at[d * 2 + e],
+            recv_sem=z_recv.at[d * 2 + e],
             device_id=(s ^ e, c ^ d),
             device_id_type=MESH,
         )
 
     for d, e in near:
-        for a in range(4):
-            cross(d, e, a, False).start()
-    own = [
-        pltpu.make_async_copy(inputs[a].at[:, columns(c, half)], held.at[s, c, a], own_sem.at[a])
-        for a in range(4)
-    ]
-    for copy in own:
-        copy.start()
+        cross(d, e, False).start()
+    own = pltpu.make_async_copy(source.at[c, half], held.at[s, c], own_sem)
+    own.start()
     swap = pltpu.make_async_remote_copy(
-        src_ref=filt.at[:, :, :, :, columns(0, half ^ 1)],
+        src_ref=filt.at[:, :, :, :, pl.ds(pl.multiple_of((half ^ 1) * lanes, lanes), lanes)],
         dst_ref=other,
         send_sem=f_send,
         recv_sem=f_recv,
@@ -101,11 +91,10 @@
                     piece(d, pair ^ mask, mask, pair).wait_recv()
                 else:
                     for e in range(2):
-                        for a in range(4):
-                            if d or e:
-                                cross(d, e, a, True).wait_recv()
-                            else:
-                                own[a].wait()
+                        if d or e:
+                            cross(d, e, True).wait_recv()
+                        else:
+                            own.wait()
                 for b in later:
                     copy = piece(d, pair ^ mask, mask ^ (1 << b), pair ^ (1 << b))
                     copy.start()
@@ -116,28 +105,47 @@
         piece(d, pair ^ mask, mask, pair).wait_recv()
     swap.wait_recv()
     for d, e in near:
-        for a in range(4):
-            cross(d, e, a, False).wait_send()
+        cross(d, e, False).wait_send()
     for copy in sent:
         copy.wait_send()
     swap.wait_send()
 
 
-def gather(inputs, filt, shards, groups):
+def arrange_kernel(*refs):
+    lanes = refs[4].shape[-1]
+    for side in range(2):
+        for a in range(4):
+            refs[4][0, side, a] = refs[a][:, side * lanes : (side + 1) * lanes]
+
+
+def arrange(inputs, groups):
     rows, channels = inputs[0].shape
-    lanes = channels // groups // 2
+    width = channels // groups
+    lanes = width // 2
+    return pl.pallas_call(
+        arrange_kernel,
+        grid=(groups,),
+        out_shape=jax.ShapeDtypeStruct((groups, 2, 4, rows, lanes), inputs[0].dtype),
+        in_specs=[pl.BlockSpec((rows, width), lambda n: (0, n))] * 4,
+        out_specs=pl.BlockSpec((1, 2, 4, rows, lanes), lambda n: (n, 0, 0, 0, 0)),
+        name="arrange",
+    )(*inputs)
+
+
+def gather(source, filt, shards):
+    groups, _, _, rows, lanes = source.shape
     return pl.pallas_call(
         functools.partial(gather_kernel, shards, groups),
         out_shape=(
-            jax.ShapeDtypeStruct((shards, groups, 4, rows, lanes), inputs[0].dtype),
+            jax.ShapeDtypeStruct((shards, groups, 4, rows, lanes), source.dtype),
             jax.ShapeDtypeStruct(filt.shape[:-1] + (lanes,), filt.dtype),
         ),
-        in_specs=[WHOLE] * 4 + [ANY],
+        in_specs=[WHOLE, ANY],
         out_specs=(ANY, ANY),
         scratch_shapes=[
-            pltpu.SemaphoreType.DMA((4,)),
-            pltpu.SemaphoreType.DMA((groups * 8,)),
-            pltpu.SemaphoreType.DMA((groups * 8,)),
+            pltpu.SemaphoreType.DMA,
+            pltpu.SemaphoreType.DMA((groups * 2,)),
+            pltpu.SemaphoreType.DMA((groups * 2,)),
             pltpu.SemaphoreType.DMA((groups * shards // 2,)),
             pltpu.SemaphoreType.DMA((groups * shards // 2,)),
             pltpu.SemaphoreType.DMA,
@@ -145,7 +153,7 @@
         ],
         compiler_params=pltpu.CompilerParams(collective_id=0, has_side_effects=True),
         name="gather",
-    )(*inputs, filt)
+    )(source, filt)
 
 
 def trade_kernel(shards, source, grad, target, other, own_sem, send_sem, recv_sem):
@@ -211,11 +219,19 @@
     peers = [(j, d) for d in range(groups - 1, -1, -1) for j in range(shards) if j or d]
     meet([(s ^ j, c ^ d) for j, d in peers])
 
+    part, lanes = source.shape[-2:]
+
+    def place(shard, group):
+        rows = pl.ds(pl.multiple_of(shard // 2 * part, part), part)
+        return target.at[
+            :, rows, pl.ds(pl.multiple_of((group * 2 + shard % 2) * lanes, lanes), lanes)
+        ]
+
     def transfer(j, d, landing):
         to_s, to_c = (s ^ j, c ^ d) if landing else (s, c)
         return pltpu.make_async_remote_copy(
             src_ref=source.at[s ^ j, c ^ d],
-            dst_ref=target.at[to_s, to_c],
+            dst_ref=place(to_s, to_c),
             send_sem=send_sem.at[d * shards + j],
             recv_sem=recv_sem.at[d * shards + j],
             device_id=(s ^ j, c ^ d),
@@ -224,7 +240,7 @@
 
     for j, d in peers:
         transfer(j, d, False).start()
-    own = pltpu.make_async_copy(source.at[s, c], target.at[s, c], own_sem)
+    own = pltpu.make_async_copy(source.at[s, c], place(s, c), own_sem)
     own.start()
     own.wait()
     for j, d in peers:
@@ -234,10 +250,12 @@
 
 
 def deliver(block):
-    shards, groups = block.shape[:2]
+    shards, groups, _, part, lanes = block.shape
     return pl.pallas_call(
         functools.partial(deliver_kernel, shards, groups),
-        out_shape=jax.ShapeDtypeStruct(block.shape, block.dtype),
+        out_shape=jax.ShapeDtypeStruct(
+            (4, part * shards // 2, groups * 2 * lanes), block.dtype
+        ),
         in_specs=[WHOLE],
         out_specs=ANY,
         scratch_shapes=[
@@ -271,6 +289,10 @@
     part = rows * 2 // shards
     step = pl.program_id(0)
     sign = (1 - 2 * side[0]).astype(jnp.float32)
+    turns = jnp.transpose(turn[0])
+
+    def twiddle(w, here):
+        return (turns[here, 2 * w : 2 * w + 1], turns[here, 2 * w + 1 : 2 * w + 2])
 
     for g in range(groups):
         here = pl.ds(g * rows, rows)
@@ -288,7 +310,7 @@
                     sums[p][0] + sums[p][1] if w == 0 else sums[p][0] - sums[p][1]
                     for p in range(2)
                 )
-                cos, sin = turn[w, 0, 0, here], turn[w, 0, 1, here]
+                cos, sin = twiddle(w, slice(g * rows, (g + 1) * rows))
                 at = (w * 2 + sig) * 2 * lanes
                 work[here, at : at + lanes] = real * cos + imag * sin
                 work[here, at + lanes : at + 2 * lanes] = imag * cos - real * sin
@@ -315,7 +337,7 @@
         by_sin = product(matrix, 2, high, low)
         real = by_cos[:, :lanes] - by_sin[:, lanes:]
         imag = by_cos[:, lanes:] + by_sin[:, :lanes]
-        cos, sin = turn[w, 0, 0] * (1.0 / total), turn[w, 0, 1] * (1.0 / total)
+        cos, sin = (table * (1.0 / total) for table in twiddle(w, slice(None)))
         found.append((real * cos - imag * sin, real * sin + imag * cos))
     for p in range(2):
         done = (found[0][p] + found[1][p], (found[0][p] - found[1][p]) * sign)
@@ -340,7 +362,7 @@
             in_specs=[
                 pl.BlockSpec(memory_space=pltpu.SMEM),
                 pl.BlockSpec((shards, groups, 4, rows, lanes), lambda n, side: (0, 0, 0, 0, 0)),
-                pl.BlockSpec((2, 1, 2, length, lanes), lambda n, side: (0, n, 0, 0, 0)),
+                pl.BlockSpec((1, 8, length), lambda n, side: (n, 0, 0)),
                 pl.BlockSpec((4, length, length), lambda n, side: (0, 0, 0)),
                 pl.BlockSpec((2, 1, 1, length, lanes), lambda n, side: (0, 0, n, 0, side[0])),
                 half_block,
@@ -387,7 +409,7 @@
     return out
 
 
-def finish_kernel(pieces, gates, result):
+def finish_kernel(pair, pieces, gates, result):
     shards, _, _, part, lanes = gates.shape
     pairs = shards // 2
     bits = pairs.bit_length() - 1
@@ -414,20 +436,24 @@
         result[i, 0, 3] = (incoming * conv).astype(jnp.bfloat16)
 
 
-def finish(pieces, gates):
-    shards, groups, _, part, lanes = gates.shape
-    gates_block = pl.BlockSpec((shards, 1, 4, part, lanes), lambda n: (0, n, 0, 0, 0))
+def finish(pair, pieces, held):
+    shards, groups, _, rows, lanes = held.shape
+    part = rows * 2 // shards
+    block = (shards, 1, 4, part, lanes)
     return pl.pallas_call(
         finish_kernel,
-        grid=(groups,),
-        out_shape=jax.ShapeDtypeStruct(gates.shape, jnp.bfloat16),
-        in_specs=[
-            pl.BlockSpec((shards // 2, 2, 2, 2, part, lanes), lambda n: (0, 0, 0, 0, n, 0)),
-            gates_block,
-        ],
-        out_specs=gates_block,
+        grid_spec=pltpu.PrefetchScalarGridSpec(
+            num_scalar_prefetch=1,
+            grid=(groups,),
+            in_specs=[
+                pl.BlockSpec((shards // 2, 2, 2, 2, part, lanes), lambda n, k: (0, 0, 0, 0, n, 0)),
+                pl.BlockSpec(block, lambda n, k: (0, n, 0, k[0], 0)),
+            ],
+            out_specs=pl.BlockSpec(block, lambda n, k: (0, n, 0, 0, 0)),
+        ),
+        out_shape=jax.ShapeDtypeStruct((shards, groups, 4, part, lanes), jnp.bfloat16),
         name="finish",
-    )(pieces, gates)
+    )(pair[None], pieces, held)
 
 
 def transform_matrix(length):
@@ -453,26 +479,18 @@
     )
     coef = jnp.stack([jnp.cos(angle), -jnp.sin(angle)], axis=1).reshape(4, shards)
     position = jnp.arange(length, dtype=jnp.int32)
-    residue = jnp.stack([own, (own + shards) % (2 * shards)])
+    residue = jnp.stack([own, (own + shards) % (2 * shards)], axis=1)
     angle = (2.0 * math.pi / total) * (residue[..., None] * position % total).astype(jnp.float32)
-    turn = jnp.stack([jnp.cos(angle), jnp.sin(angle)], axis=2)
-    turn = jnp.broadcast_to(turn[..., None], (2, 2, 2, length, 128))
-
-    held, other = gather(
-        (values_in, gate_in, gate_out, cotangent), filter_spectra, shards, groups
-    )
+    turn = jnp.stack([jnp.cos(angle), jnp.sin(angle)], axis=2).reshape(2, 4, length)
+    turn = jnp.concatenate([turn, jnp.zeros_like(turn)], axis=1)
+
+    source = arrange((values_in, gate_in, gate_out, cotangent), groups)
+    held, other = gather(source, filter_spectra, shards)
     mine, away, packed = spectral(
         side[None], coef, held, turn, transform_matrix(length), filter_spectra, other
     )
     pieces, theirs = trade(packed, away)
-    part = rows * 2 // shards
-    gates = lax.dynamic_slice_in_dim(held, index // 2 * part, part, axis=3)
-    result = deliver(finish(pieces, gates))
-    result = result.reshape((shards // 2, 2) + result.shape[1:])
-    outs = [
-        result[:, :, :, a].transpose(0, 3, 2, 1, 4).reshape(rows, values_in.shape[1])
-        for a in range(4)
-    ]
+    outs = deliver(finish(index // 2, pieces, held))
     grad_filter = jnp.concatenate(
         [jnp.where(side == 0, mine, theirs), jnp.where(side == 0, theirs, mine)], axis=-1
     )

time: 153 us -> 149 us (0.974)
  local copies, waits for them, and re-layouts: 10.1 us -> 2.82 us
  Pallas kernels: 139 us -> 142 us
    reshape x4 -> x1, local copies, waits for them, and re-layouts: 3.49 us -> 0.02 us  [on_device(): jnp.stack([jnp.cos(angle), jnp.sin(angle)], axis=2).reshape(2, 4, length)]
    pallas_call x1 -> x2, Pallas kernels: 3.97 us -> 7.38 us  [the longest x1 3.98 us: finish(): pl.pallas_call(finish_kernel, grid_spec=pltpu.PrefetchScalarGridSpec(num_...]
    transpose x5 -> x0, local copies, waits for them, and re-layouts: 2.38 us -> none  [on_device(): result[:, :, :, a].transpose(0, 3, 2, 1, 4)]
    dynamic_slice x1 -> x0, local copies, waits for them, and re-layouts: 2.32 us -> none  [on_device(): gates = lax.dynamic_slice_in_dim(held, index // 2 * part, part, axis=3)]
    squeeze x0 -> x1, local copies, waits for them, and re-layouts: none -> 2.17 us  [on_device(): return (outs[0], outs[1], outs[2], outs[3], grad_filter)]
    broadcast_in_dim x1 -> x0, local copies, waits for them, and re-layouts: 1.92 us -> none  [on_device(): turn = jnp.broadcast_to(turn[..., None], (2, 2, 2, length, 128))]
where the time goes in v3:
time: 149 us; the launch traced here: 148 us
  Pallas kernels  142 us (95%)
  local copies, waits for them, and re-layouts  2.82 us (2%)
  other arithmetic  2.76 us (2%)
    pallas_call x1, Pallas kernels, gather(): pl.pallas_call(functools.partial(gather_kernel, shards, groups), out_shap...  60.4 us
    pallas_call x1, Pallas kernels, deliver(): pl.pallas_call(functools.partial(deliver_kernel, shards, groups), out_sha...  29.9 us
    pallas_call x1, Pallas kernels, trade(): pl.pallas_call(functools.partial(trade_kernel, 2 * pairs), out_shape=(jax...  27.1 us
    pallas_call x1, Pallas kernels, spectral(): pl.pallas_call(spectral_kernel, grid_spec=pltpu.PrefetchScalarGridSpec(nu...  17 us
    pallas_call x1, Pallas kernels, finish(): pl.pallas_call(finish_kernel, grid_spec=pltpu.PrefetchScalarGridSpec(num_...  3.98 us
    pallas_call x1, Pallas kernels, arrange(): pl.pallas_call(arrange_kernel, grid=(groups,), out_shape=jax.ShapeDtypeSt...  3.4 us

profile of v3, /device:TPU:0, one launch (start us, length us, event | category | flops | bytes accessed | tf_op | source)
XLA Modules:
  0.0 148.1 jit_solution(1710592532712145466)
XLA Ops:
  0.7 0.1 pad_add_fusion
  0.8 0.1 fusion.9
  0.9 0.6 pad_maximum_fusion.2
  1.5 0.3 fusion.4
  1.9 0.6 concatenate.6.turn
  2.5 3.4 %arrange.1.refs_0_ = bf16[4,2,4,128,128]{4,3,2,1,0:T(8,128)(2,1)} custom-call(bf16[128,1024]{1,0:T(8,128)(2,1)} %refs_0_.1, bf16[128,1024]{1,0:T(8,128)(2,1)} %refs_1_.2, bf16[128,1024]{1,0:T(8,128)(2,1)} %refs_2_.1, bf16[128,1024]{1,0:T(8,128)(2,1)} %refs_3_.1), custom_call_target="tpu_custom_call" | custom-call | tf_op jit(solution)/shard_map/arrange/pallas_call | solution.py:125
  5.9 60.4 %gather.1 = (bf16[8,4,4,128,128]{4,3,2,1,0:T(8,128)(2,1)}, f32[2,1,2,512,128]{4,3,2,1,0:T(8,128)}) custom-call(bf16[4,2,4,128,128]{4,3,2,1,0:T(8,128)(2,1)} %arrange.1.refs_0_, f32[2,1,2,512,256]{4,3,2,1,0:T(8,128)} %filt.1), custom_call_target="tpu_custom_call" | custom-call | tf_op jit(solution)/shard_map/gather/pallas_call | solution.py:137
  66.3 17.0 %spectral.1 = (f32[2,1,2,512,128]{4,3,2,1,0:T(8,128)}, f32[2,1,2,512,128]{4,3,2,1,0:T(8,128)}, f32[4,2,2,2,128,128]{5,4,3,2,1,0:T(8,128)}) custom-call(s32[1]{0:T(128)} %bitcast.1.side, f32[4,8]{1,0:T(4,128)} %bitcast.11, bf16[8,4,4,128,128]{4,3,2,1,0:T(8,128)(2,1)} %get-tuple-element.12.held.gates, f32[2,8,512]{2,1,0:T(8,128)} %concatenate.6.turn, ...), custom_call_target="tpu_custom_call" | custom-call | tf_op jit(solution)/shard_map/spectral/pallas_call | solution.py:357
  83.3 27.1 %trade.1 = (f32[4,2,2,2,128,128]{5,4,3,2,1,0:T(8,128)}, f32[2,1,2,512,128]{4,3,2,1,0:T(8,128)}) custom-call(f32[4,2,2,2,128,128]{5,4,3,2,1,0:T(8,128)} %get-tuple-element.14.source, f32[2,1,2,512,128]{4,3,2,1,0:T(8,128)} %get-tuple-element.15.grad), custom_call_target="tpu_custom_call" | custom-call | tf_op jit(solution)/shard_map/trade/pallas_call | solution.py:199
  110.4 4.0 %finish.1.source = bf16[8,4,4,32,128]{4,3,2,1,0:T(8,128)(2,1)} custom-call(s32[1]{0:T(128)} %bitcast.pair, f32[4,2,2,2,128,128]{5,4,3,2,1,0:T(8,128)} %get-tuple-element.16.pieces, bf16[8,4,4,128,128]{4,3,2,1,0:T(8,128)(2,1)} %get-tuple-element.12.held.gates), custom_call_target="tpu_custom_call" | custom-call | tf_op jit(solution)/shard_map/finish/pallas_call | solution.py:443
  114.4 0.0 copy-start
  114.4 0.0 copy-start.1
  114.4 29.9 %deliver.1 = bf16[4,128,1024]{2,1,0:T(8,128)(2,1)} custom-call(bf16[8,4,4,32,128]{4,3,2,1,0:T(8,128)(2,1)} %finish.1.source), custom_call_target="tpu_custom_call" | custom-call | tf_op jit(solution)/shard_map/deliver/pallas_call | solution.py:254
  144.3 2.2 %slice_bitcast_fusion = (bf16[128,1024]{1,0:T(8,128)(2,1)}, bf16[128,1024]{1,0:T(8,128)(2,1)}, bf16[128,1024]{1,0:T(8,128)(2,1)}, bf16[128,1024]{1,0:T(8,128)(2,1)}) fusion(bf16[4,128,1024]{2,1,0:T(8,128)(2,1)} %deliver.1), kind=kLoop, calls=%fused_computation.3 | loop fusion | bytes 2097152 | tf_op jit(solution)/shard_map/squeeze | solution.py:497
  146.5 0.0 copy-done
  146.5 0.0 copy-done.1
  146.5 0.1 broadcast_select_fusion.1
  146.7 1.5 pad_maximum_fusion
  (4 shorter events, 0.1 us)
Async XLA Ops:
  114.4 32.1 %copy-start = (f32[2,1,2,512,128]{4,3,2,1,0:T(8,128)S(1)}, f32[2,1,2,512,128]{4,3,2,1,0:T(8,128)}, u32[]{:S(2)}) copy-start(f32[2,1,2,512,128]{4,3,2,1,0:T(8,128)} %get-tuple-element.17) | copy-start | bytes 3145732
  114.4 32.1 %copy-start.1 = (f32[2,1,2,512,128]{4,3,2,1,0:T(8,128)S(1)}, f32[2,1,2,512,128]{4,3,2,1,0:T(8,128)}, u32[]{:S(2)}) copy-start(f32[2,1,2,512,128]{4,3,2,1,0:T(8,128)} %get-tuple-element.18) | copy-start | bytes 3145732

commit v4 on v3

--- a/solution.py
+++ b/solution.py
@@ -75,10 +75,10 @@
 
     far = list(range(bits - 1))
     sent, landed = [], []
-    for tick in range(groups + bits):
+    for tick in range((groups + 1) // 2 * bits):
         for d in range(groups):
             order = far if d % 2 == 0 else far[::-1]
-            depth = tick - d
+            depth = tick - d // 2 * bits
             for mask in range(shards // 2):
                 if bin(mask).count("1") != depth:
                     continue

time: 149 us -> 140 us (0.940)
  Pallas kernels: 142 us -> 134 us
    pallas_call x1, Pallas kernels: 60.4 us -> 52.7 us  [gather(): pl.pallas_call(functools.partial(gather_kernel, shards, groups), out_shap...]
where the time goes in v4:
time: 140 us
  Pallas kernels  134 us (96%)
  local copies, waits for them, and re-layouts  2.82 us (2%)
  other arithmetic  2.76 us (2%)
    pallas_call x1, Pallas kernels, gather(): pl.pallas_call(functools.partial(gather_kernel, shards, groups), out_shap...  52.7 us
    pallas_call x1, Pallas kernels, deliver(): pl.pallas_call(functools.partial(deliver_kernel, shards, groups), out_sha...  29.9 us
    pallas_call x1, Pallas kernels, trade(): pl.pallas_call(functools.partial(trade_kernel, 2 * pairs), out_shape=(jax...  26.7 us
    pallas_call x1, Pallas kernels, spectral(): pl.pallas_call(spectral_kernel, grid_spec=pltpu.PrefetchScalarGridSpec(nu...  17 us
    pallas_call x1, Pallas kernels, finish(): pl.pallas_call(finish_kernel, grid_spec=pltpu.PrefetchScalarGridSpec(num_...  3.98 us
    pallas_call x1, Pallas kernels, arrange(): pl.pallas_call(arrange_kernel, grid=(groups,), out_shape=jax.ShapeDtypeSt...  3.4 us

profile of v4, /device:TPU:0, one launch (start us, length us, event | category | flops | bytes accessed | tf_op | source)
XLA Modules:
  0.0 140.0 jit_solution(6539419699690482591)
XLA Ops:
  0.7 0.1 pad_add_fusion
  0.8 0.1 fusion.9
  0.9 0.6 pad_maximum_fusion.2
  1.5 0.3 fusion.4
  1.9 0.6 concatenate.6.turn
  2.5 3.4 %arrange.1.refs_0_ = bf16[4,2,4,128,128]{4,3,2,1,0:T(8,128)(2,1)} custom-call(bf16[128,1024]{1,0:T(8,128)(2,1)} %refs_0_.1, bf16[128,1024]{1,0:T(8,128)(2,1)} %refs_1_.2, bf16[128,1024]{1,0:T(8,128)(2,1)} %refs_2_.1, bf16[128,1024]{1,0:T(8,128)(2,1)} %refs_3_.1), custom_call_target="tpu_custom_call" | custom-call | tf_op jit(solution)/shard_map/arrange/pallas_call | solution.py:125
  5.9 52.7 %gather.1 = (bf16[8,4,4,128,128]{4,3,2,1,0:T(8,128)(2,1)}, f32[2,1,2,512,128]{4,3,2,1,0:T(8,128)}) custom-call(bf16[4,2,4,128,128]{4,3,2,1,0:T(8,128)(2,1)} %arrange.1.refs_0_, f32[2,1,2,512,256]{4,3,2,1,0:T(8,128)} %filt.1), custom_call_target="tpu_custom_call" | custom-call | tf_op jit(solution)/shard_map/gather/pallas_call | solution.py:137
  58.6 17.0 %spectral.1 = (f32[2,1,2,512,128]{4,3,2,1,0:T(8,128)}, f32[2,1,2,512,128]{4,3,2,1,0:T(8,128)}, f32[4,2,2,2,128,128]{5,4,3,2,1,0:T(8,128)}) custom-call(s32[1]{0:T(128)} %bitcast.1.side, f32[4,8]{1,0:T(4,128)} %bitcast.11, bf16[8,4,4,128,128]{4,3,2,1,0:T(8,128)(2,1)} %get-tuple-element.12.held.gates, f32[2,8,512]{2,1,0:T(8,128)} %concatenate.6.turn, ...), custom_call_target="tpu_custom_call" | custom-call | tf_op jit(solution)/shard_map/spectral/pallas_call | solution.py:357
  75.6 26.7 %trade.1 = (f32[4,2,2,2,128,128]{5,4,3,2,1,0:T(8,128)}, f32[2,1,2,512,128]{4,3,2,1,0:T(8,128)}) custom-call(f32[4,2,2,2,128,128]{5,4,3,2,1,0:T(8,128)} %get-tuple-element.14.source, f32[2,1,2,512,128]{4,3,2,1,0:T(8,128)} %get-tuple-element.15.grad), custom_call_target="tpu_custom_call" | custom-call | tf_op jit(solution)/shard_map/trade/pallas_call | solution.py:199
  102.3 4.0 %finish.1.source = bf16[8,4,4,32,128]{4,3,2,1,0:T(8,128)(2,1)} custom-call(s32[1]{0:T(128)} %bitcast.pair, f32[4,2,2,2,128,128]{5,4,3,2,1,0:T(8,128)} %get-tuple-element.16.pieces, bf16[8,4,4,128,128]{4,3,2,1,0:T(8,128)(2,1)} %get-tuple-element.12.held.gates), custom_call_target="tpu_custom_call" | custom-call | tf_op jit(solution)/shard_map/finish/pallas_call | solution.py:443
  106.2 0.0 copy-start
  106.3 0.0 copy-start.1
  106.3 29.9 %deliver.1 = bf16[4,128,1024]{2,1,0:T(8,128)(2,1)} custom-call(bf16[8,4,4,32,128]{4,3,2,1,0:T(8,128)(2,1)} %finish.1.source), custom_call_target="tpu_custom_call" | custom-call | tf_op jit(solution)/shard_map/deliver/pallas_call | solution.py:254
  136.2 2.2 %slice_bitcast_fusion = (bf16[128,1024]{1,0:T(8,128)(2,1)}, bf16[128,1024]{1,0:T(8,128)(2,1)}, bf16[128,1024]{1,0:T(8,128)(2,1)}, bf16[128,1024]{1,0:T(8,128)(2,1)}) fusion(bf16[4,128,1024]{2,1,0:T(8,128)(2,1)} %deliver.1), kind=kLoop, calls=%fused_computation.3 | loop fusion | bytes 2097152 | tf_op jit(solution)/shard_map/squeeze | solution.py:497
  138.4 0.0 copy-done
  138.4 0.0 copy-done.1
  138.4 0.1 broadcast_select_fusion.1
  138.5 1.5 %pad_maximum_fusion = f32[2,1,2,512,256]{4,3,2,1,0:T(8,128)} fusion(f32[2,1,2,512,128]{4,3,2,1,0:T(8,128)S(1)} %get-tuple-element.20, f32[2,1,2,512,128]{4,3,2,1,0:T(8,128)S(1)} %get-tuple-element.19), kind=kLoop, calls=%fused_computation | loop fusion | flops 524288 | bytes 4194304 | tf_op jit(solution)/shard_map/concatenate | solution.py:494
  (4 shorter events, 0.1 us)
Async XLA Ops:
  106.2 32.1 %copy-start = (f32[2,1,2,512,128]{4,3,2,1,0:T(8,128)S(1)}, f32[2,1,2,512,128]{4,3,2,1,0:T(8,128)}, u32[]{:S(2)}) copy-start(f32[2,1,2,512,128]{4,3,2,1,0:T(8,128)} %get-tuple-element.17) | copy-start | bytes 3145732
  106.3 32.1 %copy-start.1 = (f32[2,1,2,512,128]{4,3,2,1,0:T(8,128)S(1)}, f32[2,1,2,512,128]{4,3,2,1,0:T(8,128)}, u32[]{:S(2)}) copy-start(f32[2,1,2,512,128]{4,3,2,1,0:T(8,128)} %get-tuple-element.18) | copy-start | bytes 3145732
